TPU v7x, 32 devices: a whole 2x2x4 slice. The times are simulated.
32 devices in a mesh: grp: 2 (over x), gx: 16 (over z, y, core).
Axes of the slice: x: 2, y: 2, z: 4, core: 2. Of those that a mesh axis runs over, the one named last changes fastest.
Arguments:
- pressure: float32 [256, 1024, 1024], P(('grp', 'gx')), parts along dimension 0, may hold values from -6 to 6
- centres: int32 [8], replicated, may hold values from 1 to 63
- strides: int32 [8], replicated, may hold values from 1 to 127
- kept_bins: int32 [256], replicated, may hold values from 0 to 1023, as said below
Outputs:
- spectrum: float32 [16, 1024, 256], P('grp', 'gx'), parts along dimension 0
There are 2 independent parts, one for each index of `grp`. A program takes and returns all parts, laid end to end along the dimension named above; an argument that names none is the same for every part. Nothing has to cross between parts.
Inputs may be any that keep to these rules, and one draw needn't show every extreme that they name: `kept_bins`: 256 distinct bins, among them 0 and 1023.
All inputs are finite; a program needn't handle non-finite values.
Results may differ from a plain program's by a relative error of at most 0.000092.
Values sent between devices are 32-bit elements; how exact they have to be, the bound alone decides.
No kernel may reach another device: no remote copies, remote signals or barrier semaphores. Data moves between devices by JAX's collectives and lax.ppermute only.
A program may use at most 256 MiB of HBM per device.

v0:
```python
import math

import jax
import jax.numpy as jnp
from jax import lax
from jax.sharding import PartitionSpec as P

SNAPS = 128
NX = 1024
NY = 1024
KY = 256
TAPS = 31
BANDS = 8
OUTS = 4


def partner_2(value, axis, distance):
    return lax.ppermute(value, axis, [(i, i ^ 1 << distance) for i in range(lax.axis_size(axis))])


def filter_bank(centres, strides):
    tap_index = jnp.arange(TAPS, dtype=jnp.int32)
    window = 0.5 - 0.5 * jnp.cos(2.0 * math.pi * (tap_index.astype(jnp.float32) + 1.0) / (TAPS + 1))
    phase_index = centres[:, None] * tap_index[None, :] % SNAPS
    phase_angle = -2.0 * math.pi * phase_index.astype(jnp.float32) / SNAPS
    tap_real = window[None, :] * jnp.cos(phase_angle)
    tap_imag = window[None, :] * jnp.sin(phase_angle)
    outputs = jnp.arange(OUTS, dtype=jnp.int32)
    source = (outputs[None, :, None] * strides[:, None, None] + tap_index[None, None, :]) % SNAPS
    onehot = (source[..., None] == jnp.arange(SNAPS, dtype=jnp.int32)).astype(jnp.float32)
    bank_real = jnp.einsum("bk,bjkt->bjt", tap_real, onehot, precision=lax.Precision.HIGHEST)
    bank_imag = jnp.einsum("bk,bjkt->bjt", tap_imag, onehot, precision=lax.Precision.HIGHEST)
    return (bank_real.reshape(BANDS * OUTS, SNAPS), bank_imag.reshape(BANDS * OUTS, SNAPS), window)


def bin_tables(kept_bins):
    columns = jnp.arange(NY, dtype=jnp.int32)
    phase_index = columns[:, None] * kept_bins[None, :] % NY
    phase_angle = 2.0 * math.pi * phase_index.astype(jnp.float32) / NY
    return jnp.concatenate([jnp.cos(phase_angle), jnp.sin(phase_angle)], axis=1)


def reverse_bits(number, bit_count):
    result = jnp.zeros_like(number)
    for level_bit in range(bit_count):
        result = result + (number >> level_bit & 1) * (1 << bit_count - 1 - level_bit)
    return result


def residue_rows(values_in, row_dim, groups):
    old_shape = values_in.shape
    bit_count = groups.bit_length() - 1
    local_rows = old_shape[row_dim] // groups
    new_shape = old_shape[:row_dim] + (local_rows,) + (2,) * bit_count + old_shape[row_dim + 1 :]
    axis_order = (
        list(range(row_dim))
        + list(range(row_dim + bit_count, row_dim - 1, -1))
        + list(range(row_dim + bit_count + 1, len(new_shape)))
    )
    return values_in.reshape(new_shape).transpose(axis_order).reshape(old_shape)


def rotate(spectra_field, cosine, sine):
    return jnp.stack(
        [
            spectra_field[0] * cosine - spectra_field[1] * sine,
            spectra_field[0] * sine + spectra_field[1] * cosine,
        ],
        0,
    )


def cross_rows(spectra_field, groups, device_rank, local_rows):
    bit_count = groups.bit_length() - 1
    local_index = jnp.arange(local_rows, dtype=jnp.int32)
    row_angle = (
        -2.0
        * math.pi
        * (local_index[:, None] * local_index[None, :] % local_rows).astype(jnp.float32)
        / local_rows
    )
    cosine_rows = jnp.cos(row_angle)
    sine_rows = jnp.sin(row_angle)
    with_cosine = jnp.einsum(
        "rm,csrk->csmk", cosine_rows, spectra_field, precision=lax.Precision.HIGHEST
    )
    with_sine = jnp.einsum(
        "rm,csrk->csmk", sine_rows, spectra_field, precision=lax.Precision.HIGHEST
    )
    spectra_field = jnp.stack([with_cosine[0] - with_sine[1], with_sine[0] + with_cosine[1]], 0)
    residue = reverse_bits(device_rank, bit_count)
    twist_angle = -2.0 * math.pi * (residue * local_index % NX).astype(jnp.float32) / NX
    spectra_field = rotate(
        spectra_field, jnp.cos(twist_angle)[None, :, None], jnp.sin(twist_angle)[None, :, None]
    )
    for level_bit in range(bit_count):
        partner = partner_2(spectra_field, "gx", level_bit)
        half_span = 1 << level_bit
        offset = device_rank % half_span
        step_angle = -math.pi * offset.astype(jnp.float32) / half_span
        step_cosine = jnp.cos(step_angle)
        step_sine = jnp.sin(step_angle)
        lower_side = device_rank >> level_bit & 1 == 0
        spectra_field = jnp.where(
            lower_side,
            spectra_field + rotate(partner, step_cosine, step_sine),
            partner - rotate(spectra_field, step_cosine, step_sine),
        )
    return spectra_field


def body(pressure, centres, strides, kept_bins):
    groups = lax.axis_size("gx")
    device_rank = lax.axis_index("gx")
    local_rows = NX // groups
    bank_real, bank_imag, window = filter_bank(centres, strides)
    wsum = jnp.sum(window * window)
    tables = bin_tables(kept_bins)
    stacked_bank = jnp.concatenate([bank_real, bank_imag], 0)
    signal_count = BANDS * OUTS
    shuffled = residue_rows(pressure, 1, groups)
    records = lax.all_to_all(shuffled, "gx", split_axis=1, concat_axis=0, tiled=True)
    banded = jnp.dot(
        stacked_bank,
        records.reshape(SNAPS, local_rows * NY),
        precision=lax.Precision.HIGHEST,
        preferred_element_type=jnp.float32,
    )
    projected = jnp.dot(
        banded.reshape(2 * signal_count * local_rows, NY),
        tables,
        precision=lax.Precision.HIGHEST,
        preferred_element_type=jnp.float32,
    )
    projected = projected.reshape(2, signal_count, local_rows, 2 * KY)
    real_part = projected[0, :, :, :KY] + projected[1, :, :, KY:]
    imag_part = projected[1, :, :, :KY] - projected[0, :, :, KY:]
    spectra_field = cross_rows(
        jnp.stack([real_part, imag_part], 0), groups, device_rank, local_rows
    )
    energy = spectra_field[0] * spectra_field[0] + spectra_field[1] * spectra_field[1]
    energy = energy.reshape(BANDS, OUTS, local_rows, KY)
    return jnp.mean(energy, axis=1) / (NX * NY * wsum)


def solution(mesh):
    return jax.shard_map(
        body,
        mesh=mesh,
        in_specs=(P(("grp", "gx"), None, None), P(), P(), P()),
        out_specs=P("grp", "gx", None),
        check_vma=False,
    )
```

profile of v0, /device:TPU:0, one launch (start us, length us, event | category | flops | bytes accessed | tf_op | source)
XLA Modules:
  0.0 1422.9 jit_solution(15527722153616620082)
XLA Ops:
  0.0 31.8 %copy.11 = f32[8,1024,1024]{2,0,1:T(8,128)} copy(f32[8,1024,1024]{2,1,0:T(8,128)} %param.4) | data formatting | bytes 67108864 | tf_op args[0]
  31.8 28.3 %copy.12 = f32[8,2,2,2,2,64,1024]{6,5,4,3,2,1,0:T(8,128)S(1)} copy(f32[8,2,2,2,2,64,1024]{6,0,1,2,3,4,5:T(8,128)} %bitcast.63) | data formatting | bytes 67108864 | tf_op jit(solution)/shard_map/transpose | solution.py:60
  60.1 39.9 %copy.13 = f32[8,1024,1024]{2,0,1:T(8,128)} copy(f32[8,1024,1024]{2,1,0:T(8,128)S(1)} %bitcast.60) | data formatting | bytes 67108864 | tf_op jit(solution)/shard_map/reshape | solution.py:60
  100.0 7.6 all-to-all-start
  107.7 0.1 fusion.47
  107.7 0.1 iota_multiply_fusion
  107.8 0.1 cosine_multiply_fusion
  107.9 0.1 add_select_fusion.2
  108.0 0.4 fusion.22
  108.4 0.4 fusion.21
  108.8 4.1 fusion.20
  112.9 583.4 %all-to-all-done = f32[8,1024,1024]{2,0,1:T(8,128)} async-done(((f32[8,1024,1024]{2,0,1:T(8,128)}), f32[8,1024,1024]{2,0,1:T(8,128)}, u32[]{:S(2)}, u32[]{:S(2)}) %all-to-all-start) | async-done | bytes 33554464 | tf_op jit(solution)/shard_map/all_to_all | solution.py:122
  696.4 28.2 %copy.29 = f32[8,16,64,1024]{3,2,0,1:T(8,128)S(1)} copy(f32[8,16,64,1024]{3,0,2,1:T(8,128)} %bitcast.16) | data formatting | bytes 67108864 | tf_op jit(solution)/shard_map/all_to_all | solution.py:122
  724.6 21.5 %copy.25 = f32[16,8,64,1024]{3,1,2,0:T(8,128)} copy(f32[16,8,64,1024]{3,2,1,0:T(8,128)S(1)} %bitcast.61) | data formatting | bytes 67108864
  746.1 33.4 %copy.15 = f32[65536,128]{1,0:T(8,128)} copy(f32[65536,128]{0,1:T(8,128)} %bitcast.62) | data formatting | bytes 67108864 | tf_op jit(solution)/shard_map/dot_general | solution.py:123
  779.5 44.2 %fusion.60 = f32[2,32,64,1024]{3,1,2,0:T(8,128)} fusion(f32[2,32,128,1]{2,1,3,0:T(8,128)S(1)} %bitcast.65, f32[64,1024,128,1]{2,1,0,3:T(8,128)} %bitcast.59), kind=kOutput, calls=%fused_computation.117 | convolution fusion | flops 6442450944 | bytes 50364416 | tf_op jit(solution)/shard_map/dot_general | solution.py:123
  823.7 39.9 %fusion = f32[2,32,64,512]{3,2,1,0:T(8,128)S(1)} fusion(f32[2,32,64,1024]{3,1,2,0:T(8,128)} %fusion.60, f32[1024,256]{1,0:T(8,128)S(1)} %get-tuple-element.25, f32[1024,256]{1,0:T(8,128)S(1)} %get-tuple-element.24), kind=kOutput, calls=%fused_computation.1 | convolution fusion | flops 25770328064 | bytes 27262976 | tf_op jit(solution)/shard_map/dot_general | solution.py:129
  863.6 0.8 slice_add_fusion.1
  864.4 4.1 fusion.9
  868.5 4.2 fusion.8
  872.7 2.8 multiply_subtract_fusion.6
  875.5 2.6 pad_maximum_fusion.1
  878.1 1.0 collective-permute-start
  879.1 1.9 multiply_add_fusion.6
  881.0 0.0 copy-start.3
  881.0 0.0 copy-start.1
  881.0 5.2 collective-permute-done
  886.2 2.7 multiply_subtract_fusion.7
  888.9 6.3 fusion.2
  895.2 45.6 %collective-permute-start.1 = (f32[2,32,64,256]{3,2,1,0:T(8,128)}, f32[2,32,64,256]{3,2,1,0:T(8,128)}, u32[]{:S(2)}, u32[]{:S(2)}) collective-permute-start(f32[2,32,64,256]{3,2,1,0:T(8,128)} %fusion.2), channel_id=1, source_target_pairs={{0,2},{1,3},{2,0},{3,1},{4,6},{5,7},{6,4},{7,5},{8,10},{9,11},{10,... | collective-permute-start | bytes 12582920 | tf_op jit(solution)/shard_map/ppermute | solution.py:18
  941.0 3.0 multiply_subtract_fusion.4
  944.0 88.2 %collective-permute-done.1 = f32[2,32,64,256]{3,2,1,0:T(8,128)} collective-permute-done((f32[2,32,64,256]{3,2,1,0:T(8,128)}, f32[2,32,64,256]{3,2,1,0:T(8,128)}, u32[]{:S(2)}, u32[]{:S(2)}) %collective-permute-start.1) | collective-permute-done | bytes 4194336 | tf_op jit(solution)/shard_map/ppermute | solution.py:18
  1032.2 2.8 multiply_subtract_fusion.5
  1035.1 6.9 fusion.3
  1042.0 89.9 %collective-permute-start.2 = (f32[2,32,64,256]{3,2,1,0:T(8,128)}, f32[2,32,64,256]{3,2,1,0:T(8,128)}, u32[]{:S(2)}, u32[]{:S(2)}) collective-permute-start(f32[2,32,64,256]{3,2,1,0:T(8,128)} %fusion.3), channel_id=1, source_target_pairs={{0,4},{1,5},{2,6},{3,7},{4,0},{5,1},{6,2},{7,3},{8,12},{9,13},{10,... | collective-permute-start | bytes 12582920 | tf_op jit(solution)/shard_map/ppermute | solution.py:18
  1132.0 2.8 multiply_subtract_fusion.2
  1134.8 87.9 %collective-permute-done.2 = f32[2,32,64,256]{3,2,1,0:T(8,128)} collective-permute-done((f32[2,32,64,256]{3,2,1,0:T(8,128)}, f32[2,32,64,256]{3,2,1,0:T(8,128)}, u32[]{:S(2)}, u32[]{:S(2)}) %collective-permute-start.2) | collective-permute-done | bytes 4194336 | tf_op jit(solution)/shard_map/ppermute | solution.py:18
  1222.7 2.8 multiply_subtract_fusion.3
  1225.5 5.6 fusion.4
  1231.1 2.6 collective-permute-start.3
  1233.9 0.7 multiply_reduce_fusion
  1235.2 2.8 multiply_subtract_fusion
  1238.0 175.9 %collective-permute-done.3 = f32[2,32,64,256]{3,2,1,0:T(8,128)} collective-permute-done((f32[2,32,64,256]{3,2,1,0:T(8,128)}, f32[2,32,64,256]{3,2,1,0:T(8,128)}, u32[]{:S(2)}, u32[]{:S(2)}) %collective-permute-start.3) | collective-permute-done | bytes 4194336 | tf_op jit(solution)/shard_map/ppermute | solution.py:18
  1413.9 2.8 multiply_subtract_fusion.1
  1416.7 4.3 fusion.5
  1421.1 0.3 fusion.10
  1421.4 0.2 reduce_sum.18
  1421.6 0.9 multiply_divide_fusion
  (28 shorter events, 0.1 us)
Async XLA Ops:
  100.0 7.7 copy-start.12
  100.0 7.8 copy-start.13
  100.0 8.8 copy-start.11
  100.0 596.4 %all-to-all-start = ((f32[8,1024,1024]{2,0,1:T(8,128)}), f32[8,1024,1024]{2,0,1:T(8,128)}, u32[]{:S(2)}, u32[]{:S(2)}) async-start(f32[8,1024,1024]{2,0,1:T(8,128)} %copy.13), calls=%async_computation | async-start | bytes 67108864 | tf_op jit(solution)/shard_map/all_to_all | solution.py:122
  875.5 2.7 copy-start
  878.1 8.1 collective-permute-start
  881.0 7.9 copy-start.3
  881.0 7.9 copy-start.1
  881.0 7.9 copy-start.9
  888.9 6.3 copy-start.5
  888.9 6.3 copy-start.7
  895.2 137.0 %collective-permute-start.1 = (f32[2,32,64,256]{3,2,1,0:T(8,128)}, f32[2,32,64,256]{3,2,1,0:T(8,128)}, u32[]{:S(2)}, u32[]{:S(2)}) collective-permute-start(f32[2,32,64,256]{3,2,1,0:T(8,128)} %fusion.2), channel_id=1, source_target_pairs={{0,2},{1,3},{2,0},{3,1},{4,6},{5,7},{6,4},{7,5},{8,10},{9,11},{10,... | collective-permute-start | bytes 12582920 | tf_op jit(solution)/shard_map/ppermute | solution.py:18
  941.0 94.1 %copy-start.10 = (f32[1,32,64,256]{3,2,1,0:T(8,128)S(1)}, f32[1,32,64,256]{3,2,1,0:T(8,128)}, u32[]{:S(2)}) copy-start(f32[1,32,64,256]{3,2,1,0:T(8,128)} %get-tuple-element.5) | copy-start | bytes 6291460
  944.0 91.1 %copy-start.2 = (f32[1,32,64,256]{3,2,1,0:T(8,128)S(1)}, f32[1,32,64,256]{3,2,1,0:T(8,128)}, u32[]{:S(2)}) copy-start(f32[1,32,64,256]{3,2,1,0:T(8,128)} %copy-done) | copy-start | bytes 6291460
  944.0 91.1 %copy-start.4 = (f32[1,32,64,256]{3,2,1,0:T(8,128)S(1)}, f32[1,32,64,256]{3,2,1,0:T(8,128)}, u32[]{:S(2)}) copy-start(f32[1,32,64,256]{3,2,1,0:T(8,128)} %copy-done.3) | copy-start | bytes 6291460
  944.0 91.1 %copy-start.6 = (f32[1,32,64,256]{3,2,1,0:T(8,128)S(1)}, f32[1,32,64,256]{3,2,1,0:T(8,128)}, u32[]{:S(2)}) copy-start(f32[1,32,64,256]{3,2,1,0:T(8,128)} %copy-done.5) | copy-start | bytes 6291460
  944.0 91.1 %copy-start.8 = (f32[1,32,64,256]{3,2,1,0:T(8,128)S(1)}, f32[1,32,64,256]{3,2,1,0:T(8,128)}, u32[]{:S(2)}) copy-start(f32[1,32,64,256]{3,2,1,0:T(8,128)} %copy-done.7) | copy-start | bytes 6291460
  1042.0 180.7 %collective-permute-start.2 = (f32[2,32,64,256]{3,2,1,0:T(8,128)}, f32[2,32,64,256]{3,2,1,0:T(8,128)}, u32[]{:S(2)}, u32[]{:S(2)}) collective-permute-start(f32[2,32,64,256]{3,2,1,0:T(8,128)} %fusion.3), channel_id=1, source_target_pairs={{0,4},{1,5},{2,6},{3,7},{4,0},{5,1},{6,2},{7,3},{8,12},{9,13},{10,... | collective-permute-start | bytes 12582920 | tf_op jit(solution)/shard_map/ppermute | solution.py:18
  1231.1 182.8 %collective-permute-start.3 = (f32[2,32,64,256]{3,2,1,0:T(8,128)}, f32[2,32,64,256]{3,2,1,0:T(8,128)}, u32[]{:S(2)}, u32[]{:S(2)}) collective-permute-start(f32[2,32,64,256]{3,2,1,0:T(8,128)} %fusion.4), channel_id=1, source_target_pairs={{0,8},{1,9},{2,10},{3,11},{4,12},{5,13},{6,14},{7,15},{8,0},{9,1},... | collective-permute-start | bytes 12582920 | tf_op jit(solution)/shard_map/ppermute | solution.py:18
where the time goes:
time: 1430 us; the launch traced here: 1420 us
  waiting for transfers between devices  941 us (66%)
  local copies, waits for them, and re-layouts  183 us (13%)
  starting transfers between devices  147 us (10%)
  matrix products  93.2 us (7%)
  other arithmetic  57.3 us (4%)
    all_to_all x1, waiting for transfers between devices, body(): lax.all_to_all(shuffled, 'gx', split_axis=1, concat_axis=0, tiled=True)  583 us
    ppermute x4, waiting for transfers between devices, partner_2(): lax.ppermute(value, axis, [(i, i ^ 1 << distance) for i in range(lax.axis...  357 us
    ppermute x4, starting transfers between devices, partner_2(): lax.ppermute(value, axis, [(i, i ^ 1 << distance) for i in range(lax.axis...  139 us
    unnamed x30, local copies, waits for them, and re-layouts  53.4 us
    dot_general x1, matrix products, body(): jnp.dot(stacked_bank, records.reshape(SNAPS, local_rows * NY), precision=...  44.2 us
    reshape x1, local copies, waits for them, and re-layouts, residue_rows(): return values_in.reshape(new_shape).transpose(axis_order).reshape(old_shape)  39.9 us
    dot_general x1, matrix products, body(): jnp.dot(banded.reshape(2 * signal_count * local_rows, NY), tables, precis...  39.9 us
    dot_general x1, local copies, waits for them, and re-layouts, body(): jnp.dot(stacked_bank, records.reshape(SNAPS, local_rows * NY), precision=...  33.4 us
  transfers between devices with their start and end apart: 5, of which 5 were waited for; matrix products, arithmetic and copies ran while one was open for 1% of the time, Pallas kernels for 0%

commit v1 on v0

v1 whole, which is shorter than its diff:
```python
import functools
import math

import jax
import jax.numpy as jnp
import numpy as np
from jax import lax
from jax.experimental import pallas as pl
from jax.experimental.pallas import tpu as pltpu
from jax.sharding import PartitionSpec as P

KY = 256
TAPS = 31
BANDS = 8
OUTS = 4
LANES = 128
BINS = LANES // 2


def split_bf16(values):
    high = values.astype(jnp.bfloat16)
    low = (values - high.astype(jnp.float32)).astype(jnp.bfloat16)
    return high, low


def split_exact(values):
    high = lax.reduce_precision(values, 8, 7)
    return high.astype(jnp.bfloat16), (values - high).astype(jnp.bfloat16)


def split_host(values):
    values = values.astype(np.float32)
    high = values.astype(jnp.bfloat16)
    low = (values - high.astype(np.float32)).astype(jnp.bfloat16)
    return high, low


def times_i(values):
    lane = lax.broadcasted_iota(jnp.int32, values.shape, 1)
    turned = pltpu.roll(values, BINS, 1)
    return jnp.where(lane < BINS, -turned, turned)


def dot32(left, right):
    return jnp.dot(left, right, preferred_element_type=jnp.float32)


def transform_kernel(radix, share, groups, rank_ref, p_ref, factor_ref, mh_ref, ml_ref, twc_ref, tws_ref, *rest):
    outs, (table_ref, g_ref, f_ref) = rest[:-3], rest[-3:]
    half = groups // 2
    parts = len(outs) // half
    rows = p_ref.shape[1]
    span = rows // radix
    block = 256
    fine = factor_ref.shape[1]

    @pl.when(pl.program_id(0) == 0)
    def _():
        for a in range(p_ref.shape[2] // fine):
            at = slice(a, a + 1)
            both = factor_ref[0, at, :] * factor_ref[2] - factor_ref[1, at, :] * factor_ref[3]
            high, low = split_bf16(both)
            table_ref[a * fine : (a + 1) * fine, :] = jnp.concatenate([high, low], 1)

    @pl.loop(0, rows // block)
    def _(r):
        at = pl.ds(pl.multiple_of(r * block, block), block)
        high, low = split_bf16(p_ref[0, at, :])
        both = dot32(high, table_ref[...]) + dot32(low, table_ref[...])
        g_ref[at, :] = both[:, :LANES] + both[:, LANES:]

    fields = [g_ref[r * span : (r + 1) * span, :] for r in range(radix)]
    if radix == 4:
        a, b = fields[0] + fields[2], fields[0] - fields[2]
        c, d = fields[1] + fields[3], times_i(fields[1] - fields[3])
        fields = [a + c, b - d, a - c, b + d]
    elif radix == 2:
        fields = [fields[0] + fields[1], fields[0] - fields[1]]
    for s, field in enumerate(fields):
        if s:
            field = twc_ref[s] * field + tws_ref[s] * times_i(field)
        high, low = split_bf16(jnp.concatenate([field, times_i(field)], 0))
        right = jnp.concatenate([high, low], 1)
        both = dot32(mh_ref[...], right) + dot32(ml_ref[...], right)
        f_ref[s] = both[:, :LANES] + both[:, LANES:]
    steps = radix // parts
    for k in range(half):
        for h in range(2):
            at = pl.ds(pl.multiple_of((rank_ref[0] ^ (k + h * half)) * share, share), share)
            for s in range(radix):
                first = (h * steps + s % steps) * share
                outs[s // steps * half + k][0, first : first + share, :] = f_ref[s, at, :]


def filter_kernel(places, bank_ref, *rest):
    pieces, out, x_ref = rest[:-2], rest[-2], rest[-1]
    signals, rows = out.shape[1], out.shape[0]
    snaps = x_ref.shape[0] // rows
    for place, piece in zip(places, pieces):
        for t in range(piece.shape[0]):
            first = (place + t) * rows
            x_ref[first : first + rows, :] = piece[t]
    for r in range(rows):
        field = x_ref[pl.ds(r, snaps, stride=rows), :]
        high, low = split_bf16(jnp.concatenate([field, times_i(field)], 0))
        both = dot32(bank_ref[...], jnp.concatenate([high, low], 1))
        both = both[:, :LANES] + both[:, LANES:]
        out[r] = both[:signals] + both[signals:]


def energy_kernel(radix, share, counts, held, scale_ref, *rest):
    fields, out, e_ref = rest[held:-2], rest[-2], rest[-1]
    sides = (fields[: counts[0]], fields[counts[0] :])
    rows = out.shape[1]
    for s in range(radix):
        for i in range(share):
            row = s * share + i
            powers = []
            for side in sides:
                size = side[0].shape[0]
                own, other = side[row // size * 2 : row // size * 2 + 2]
                field = own[row % size] + other[row % size]
                power = field * field
                total = power[:BANDS]
                for j in range(1, OUTS):
                    total = total + power[j * BANDS : (j + 1) * BANDS]
                powers.append(total + pltpu.roll(total, BINS, 1))
            lane = lax.broadcasted_iota(jnp.int32, powers[0].shape, 1)
            x = i * radix + s
            e_ref[x * BANDS : (x + 1) * BANDS, :] = scale_ref[0] * jnp.where(
                lane < BINS, powers[0], powers[1]
            )
    for b in range(BANDS):
        out[b, :, :] = e_ref[pl.ds(b, rows, stride=BANDS), :]


def filter_bank(centres, strides, snaps, times):
    tap_index = jnp.arange(TAPS, dtype=jnp.int32)
    window = 0.5 - 0.5 * jnp.cos(2.0 * math.pi * (tap_index.astype(jnp.float32) + 1.0) / (TAPS + 1))
    phase_index = centres[:, None] * tap_index[None, :] % snaps
    phase_angle = -2.0 * math.pi * phase_index.astype(jnp.float32) / snaps
    tap_real = window[None, :] * jnp.cos(phase_angle)
    tap_imag = window[None, :] * jnp.sin(phase_angle)
    outputs = jnp.arange(OUTS, dtype=jnp.int32)
    source = (outputs[:, None, None] * strides[None, :, None] + tap_index[None, None, :]) % snaps
    chosen = source[..., None] == times
    bank_real = jnp.sum(jnp.where(chosen, tap_real[None, :, :, None], 0.0), axis=2)
    bank_imag = jnp.sum(jnp.where(chosen, tap_imag[None, :, :, None], 0.0), axis=2)
    signals = BANDS * OUTS
    bank = jnp.concatenate(
        [bank_real.reshape(signals, -1), bank_imag.reshape(signals, -1)], axis=1
    )
    return jnp.concatenate(split_exact(bank), axis=0), jnp.sum(window * window)


def bin_factors(kept_bins, ny):
    fine = 32
    lane = jnp.arange(2 * KY, dtype=jnp.int32)
    chunks = kept_bins.reshape(KY // BINS, 1, BINS)
    bins = jnp.concatenate([chunks, chunks], axis=1).reshape(2 * KY)
    quarter = (lane // BINS % 2) * (ny // 4)
    index = jnp.arange(fine, dtype=jnp.int32)[:, None]
    phase = jnp.stack([index * fine * bins, index * bins + quarter], 0) % ny
    angle = phase.astype(jnp.float32) * (2.0 * math.pi / ny)
    cosine, sine = jnp.cos(angle), jnp.sin(angle)
    return jnp.stack([cosine[0], sine[0], cosine[1], sine[1]], 0)


def body(pressure, centres, strides, kept_bins):
    groups = lax.axis_size("gx")
    rank = lax.axis_index("gx")
    local, nx, ny = pressure.shape
    snaps = local * groups
    half = groups // 2
    each = nx // groups
    radix = 4 if each >= 32 else 2 if each >= 16 else 1
    share = each // radix
    span = nx // radix
    signals = BANDS * OUTS

    partner = rank ^ jnp.arange(half, dtype=jnp.int32)
    times = (partner[:, None] * local + jnp.arange(local, dtype=jnp.int32)[None, :]).reshape(-1)
    factors = bin_factors(kept_bins, ny)
    bank, wsum = filter_bank(centres, strides, snaps, times)
    scale = (1.0 / (OUTS * nx * ny * wsum)).reshape(1)
    rank_word = rank.reshape(1).astype(jnp.int32)

    index = np.arange(span, dtype=np.int64)
    angle = 2.0 * np.pi * (index[:, None] * index[None, :] % span) / span
    mh, ml = split_host(np.concatenate([np.cos(angle), np.sin(-angle)], 1))
    twist = 2.0 * np.pi * (np.arange(radix)[:, None] * index[None, :]) / nx
    twist = np.broadcast_to(twist[:, :, None], (radix, span, LANES))
    twc, tws = np.cos(twist).astype(np.float32), np.sin(-twist).astype(np.float32)

    def whole(shape):
        return pl.BlockSpec(shape, lambda *_: (0,) * len(shape))

    def transform(c, factor, first, count, parts):
        size = 2 * each // parts
        return pl.pallas_call(
            functools.partial(transform_kernel, radix, share, groups),
            grid_spec=pltpu.PrefetchScalarGridSpec(
                num_scalar_prefetch=1,
                grid=(count,),
                in_specs=[
                    pl.BlockSpec((1, nx, ny), lambda t, _: (t + first, 0, 0)),
                    pl.BlockSpec((4, factor.shape[1], LANES), lambda t, _: (0, 0, c)),
                    whole(mh.shape),
                    whole(ml.shape),
                    whole(twc.shape),
                    whole(tws.shape),
                ],
                out_specs=[pl.BlockSpec((1, size, LANES), lambda t, _: (t, 0, 0))] * (half * parts),
                scratch_shapes=[
                    pltpu.VMEM((ny, 2 * LANES), jnp.bfloat16),
                    pltpu.VMEM((nx, LANES), jnp.float32),
                    pltpu.VMEM((radix, span, LANES), jnp.float32),
                ],
            ),
            out_shape=[jax.ShapeDtypeStruct((count, size, LANES), jnp.float32)] * (half * parts),
            cost_estimate=pl.CostEstimate(
                flops=count * (8 * nx * ny * LANES + 16 * nx * span * LANES),
                bytes_accessed=count * nx * (ny + LANES) * 4,
                transcendentals=0,
            ),
            name="transform",
        )(rank_word, pressure, factor, mh, ml, twc, tws)

    def filtered(bank, places, pieces, side):
        total = pieces[0].shape[1] // 2
        rows = min(16, total)
        blocks = total // rows
        return pl.pallas_call(
            functools.partial(filter_kernel, places),
            grid=(blocks,),
            in_specs=[whole(bank.shape)]
            + [pl.BlockSpec((x.shape[0], rows, LANES), lambda r: (0, side * blocks + r, 0)) for x in pieces],
            out_specs=pl.BlockSpec((rows, signals, LANES), lambda r: (r, 0, 0)),
            out_shape=jax.ShapeDtypeStruct((total, signals, LANES), jnp.float32),
            scratch_shapes=[pltpu.VMEM((half * local * rows, LANES), jnp.float32)],
            cost_estimate=pl.CostEstimate(
                flops=total * 16 * signals * half * local * LANES,
                bytes_accessed=total * LANES * (half * local + signals) * 4,
                transcendentals=0,
            ),
            name="filter",
        )(bank, *pieces)

    def energy(pair, counts, scale, fields, held):
        return pl.pallas_call(
            functools.partial(energy_kernel, radix, share, counts, len(held)),
            in_specs=[pl.BlockSpec(memory_space=pltpu.SMEM)]
            + [pl.BlockSpec(memory_space=pl.ANY)] * len(held)
            + [whole(x.shape) for x in fields],
            out_specs=pl.BlockSpec((BANDS, each, LANES), lambda _: (0, 0, pair)),
            out_shape=jax.ShapeDtypeStruct((BANDS, each, KY), jnp.float32),
            scratch_shapes=[pltpu.VMEM((each * BANDS, LANES), jnp.float32)],
            grid=(1,),
            input_output_aliases={1: 0} if held else {},
            name="energy",
        )(scale, *held, *fields)

    def swap(value, bits):
        return lax.ppermute(value, "gx", [(i, i ^ bits) for i in range(groups)])

    def exchange(pieces):
        moved = {k: swap(pieces[k], k) for k in reversed(range(1, half))}
        return [pieces[0]] + [moved[k] for k in range(1, half)]

    last_made = [rank_word]

    def in_turn(operand):
        return lax.optimization_barrier((operand, last_made[0]))[0]

    def project(c, pieces_per, parts):
        step = local // pieces_per
        places, found = [], [[] for _ in range(parts)]
        for n in range(pieces_per):
            made = transform(c, in_turn(factors), n * step, step, parts)
            last_made[0] = made[0]
            places += [k * local + n * step for k in range(half)]
            for q in range(parts):
                found[q] += exchange(made[q * half : (q + 1) * half])
        return [(places, pieces) for pieces in found]

    def combine(group, side):
        made = filtered(in_turn(bank), *group, side)
        last_made[0] = made
        return made

    def meet(group):
        made = combine(group, 1)
        return swap(made, half)

    halves = 2 if local % 2 == 0 else 1
    parts = 2 if radix >= 2 else 1
    (zero,) = project(0, halves, 1)
    (one,) = project(1, halves, 1)
    theirs = [meet(zero)]
    (two,) = project(2, 1, 1)
    three = project(3, 1, parts)
    theirs.append(meet(one))
    mine = [combine(zero, 0), combine(one, 0)]
    theirs.append(meet(two))
    mine.append(combine(two, 0))
    out = []
    for n, group in enumerate(three):
        theirs.append(meet(group))
        mine.append(combine(group, 0))
        if n == 0:
            fields = [mine[0], theirs[0], mine[1], theirs[1]]
            out = [energy(0, (2, 2), in_turn(scale), fields, [])]
            last_made[0] = out[0]
    fields = [x for pair in zip(mine[2:], theirs[2:]) for x in pair]
    return energy(1, (2, 2 * parts), in_turn(scale), fields, out)


def solution(mesh):
    return jax.shard_map(
        body,
        mesh=mesh,
        in_specs=(P(("grp", "gx"), None, None), P(), P(), P()),
        out_specs=P("grp", "gx", None),
        check_vma=False,
    )
```

time: 1430 us -> 406 us (0.28)
  waiting for transfers between devices: 941 us -> 179 us
  local copies, waits for them, and re-layouts: 183 us -> 6.54 us
  Pallas kernels: 0 us -> 153 us
  matrix products: 93.2 us -> 0 us
  starting transfers between devices: 147 us -> 61 us
  other arithmetic: 57.3 us -> 3.29 us
    all_to_all x1 -> x0, waiting for transfers between devices: 583 us -> none  [body(): lax.all_to_all(shuffled, 'gx', split_axis=1, concat_axis=0, tiled=True)]
    ppermute x4 -> x54, waiting for transfers between devices: 357 us -> 179 us  [swap(): return lax.ppermute(value, 'gx', [(i, i ^ bits) for i in range(groups)])]
    pallas_call x0 -> x18, Pallas kernels: none -> 153 us  [the longest x6 109 us: transform(): pl.pallas_call(functools.partial(transform_kernel, radix, share, groups),...]
    dot_general x6 -> x0, matrix products: 93.2 us -> none  [the longest x1 44.2 us: body(): jnp.dot(stacked_bank, records.reshape(SNAPS, local_rows * NY), precision=...]
    ppermute x4 -> x54, starting transfers between devices: 139 us -> 61 us  [swap(): return lax.ppermute(value, 'gx', [(i, i ^ bits) for i in range(groups)])]
    unnamed x30 -> x100, local copies, waits for them, and re-layouts: 53.4 us -> 5.43 us
    reshape x1, local copies, waits for them, and re-layouts: 39.9 us -> 0.76 us  [bin_factors(): chunks = kept_bins.reshape(KY // BINS, 1, BINS)]
    dot_general x1 -> x0, local copies, waits for them, and re-layouts: 33.4 us -> none  [body(): jnp.dot(stacked_bank, records.reshape(SNAPS, local_rows * NY), precision=...]
  transfers between devices with their start and end apart: 5 -> 54, of which waited for: 5 -> 18; matrix products, arithmetic and copies ran while one was open for 1% -> 1% of each run, Pallas kernels for 0% -> 30%
where the time goes in v1:
time: 406 us; the launch traced here: 404 us
  waiting for transfers between devices  179 us (44%)
  Pallas kernels  153 us (38%)
  starting transfers between devices  61 us (15%)
  local copies, waits for them, and re-layouts  6.54 us (2%)
    ppermute x54, waiting for transfers between devices, swap(): return lax.ppermute(value, 'gx', [(i, i ^ bits) for i in range(groups)])  179 us
    pallas_call x6, Pallas kernels, transform(): pl.pallas_call(functools.partial(transform_kernel, radix, share, groups),...  109 us
    ppermute x54, starting transfers between devices, swap(): return lax.ppermute(value, 'gx', [(i, i ^ bits) for i in range(groups)])  61 us
    pallas_call x10, Pallas kernels, filtered(): pl.pallas_call(functools.partial(filter_kernel, places), grid=(blocks,),...  37.5 us
  transfers between devices with their start and end apart: 54, of which 18 were waited for; matrix products, arithmetic and copies ran while one was open for 1% of the time, Pallas kernels for 30%

profile of v1, /device:TPU:0, one launch (start us, length us, event | category | flops | bytes accessed | tf_op | source)
XLA Modules:
  0.0 403.7 jit_solution(16941833222681810787)
XLA Ops:
  2.2 14.4 %transform.6 = (f32[4,128,128]{2,1,0:T(8,128)}, f32[4,128,128]{2,1,0:T(8,128)}, f32[4,128,128]{2,1,0:T(8,128)}, f32[4,128,128]{2,1,0:T(8,128)}, f32[4,128,128]{2...) custom-call(s32[1]{0:T(128)} %bitcast.3.rank_ref, f32[8,1024,1024]{2,1,0:T(8,128)} %p_ref.11, ...), custom_call_target="tpu_custom_call" | custom-call | flops 6442450944 | bytes 18874368 | tf_op jit(solution)/shard_map/transform/pallas_call | solution.py:200
  16.6 14.4 %transform.7 = (f32[4,128,128]{2,1,0:T(8,128)}, f32[4,128,128]{2,1,0:T(8,128)}, f32[4,128,128]{2,1,0:T(8,128)}, f32[4,128,128]{2,1,0:T(8,128)}, f32[4,128,128]{2...) custom-call(s32[1]{0:T(128)} %bitcast.3.rank_ref, f32[8,1024,1024]{2,1,0:T(8,128)} %p_ref.11, ...), custom_call_target="tpu_custom_call" | custom-call | flops 6442450944 | bytes 18874368 | tf_op jit(solution)/shard_map/transform/pallas_call | solution.py:200
  31.0 3.1 collective-permute-start.10
  34.2 2.1 collective-permute-start.12
  37.2 14.5 %transform.8 = (f32[4,128,128]{2,1,0:T(8,128)}, f32[4,128,128]{2,1,0:T(8,128)}, f32[4,128,128]{2,1,0:T(8,128)}, f32[4,128,128]{2,1,0:T(8,128)}, f32[4,128,128]{2...) custom-call(s32[1]{0:T(128)} %bitcast.3.rank_ref, f32[8,1024,1024]{2,1,0:T(8,128)} %p_ref.11, ...), custom_call_target="tpu_custom_call" | custom-call | flops 6442450944 | bytes 18874368 | tf_op jit(solution)/shard_map/transform/pallas_call | solution.py:200
  51.7 14.4 %transform.9 = (f32[4,128,128]{2,1,0:T(8,128)}, f32[4,128,128]{2,1,0:T(8,128)}, f32[4,128,128]{2,1,0:T(8,128)}, f32[4,128,128]{2,1,0:T(8,128)}, f32[4,128,128]{2...) custom-call(s32[1]{0:T(128)} %bitcast.3.rank_ref, f32[8,1024,1024]{2,1,0:T(8,128)} %p_ref.11, ...), custom_call_target="tpu_custom_call" | custom-call | flops 6442450944 | bytes 18874368 | tf_op jit(solution)/shard_map/transform/pallas_call | solution.py:200
  70.3 5.1 %collective-permute-done.8.rest_10_ = f32[4,128,128]{2,1,0:T(8,128)S(1)} collective-permute-done((f32[4,128,128]{2,1,0:T(8,128)S(1)}, f32[4,128,128]{2,1,0:T(8,128)S(1)}, u32[]{:S(2)}, u32[]{:S(2)}) %collective-permute-start.8) | collective-permute-done | bytes 262176 | tf_op jit(solution)/shard_map/ppermute | solution.py:264
  76.9 3.3 collective-permute-done.9.rest_11_
  80.1 2.1 collective-permute-start.4
  84.1 2.6 collective-permute-done.1.rest_2_
  87.7 14.3 %collective-permute-done.2.rest_3_ = f32[4,128,128]{2,1,0:T(8,128)S(1)} collective-permute-done((f32[4,128,128]{2,1,0:T(8,128)}, f32[4,128,128]{2,1,0:T(8,128)S(1)}, u32[]{:S(2)}, u32[]{:S(2)}) %collective-permute-start.2) | collective-permute-done | bytes 262176 | tf_op jit(solution)/shard_map/ppermute | solution.py:264
  107.1 4.4 %filter.10 = f32[64,32,128]{2,1,0:T(8,128)} custom-call(bf16[64,128]{1,0:T(8,128)(2,1)} %pad_maximum_fusion.2.bank_ref, f32[4,128,128]{2,1,0:T(8,128)} %get-tuple-element.80.rest_0_, f32[4,128,128]{2,1,0:T(8,128)} %copy-done.13, f32[4,128,128]{2,1,0:T(8,128)} %copy-done.14, f32[4,128,128]{2,1,0:T(8,128)} %copy-done.15, f32[4,128,128]{2,1,0:T(8,128)} %copy-done.16, ...), custom_call_target="tpu_custom_call" | custom-call | flops 268435456 | bytes 3145728 | tf_op jit(solution)/shard_map/filter/pallas_call | solution.py:233
  111.6 2.7 collective-permute-start.26
  118.6 25.3 %transform.10 = (f32[8,128,128]{2,1,0:T(8,128)}, f32[8,128,128]{2,1,0:T(8,128)}, f32[8,128,128]{2,1,0:T(8,128)}, f32[8,128,128]{2,1,0:T(8,128)}, f32[8,128,128]{...) custom-call(s32[1]{0:T(128)} %bitcast.3.rank_ref, ...), custom_call_target="tpu_custom_call" | custom-call | flops 12884901888 | bytes 37748736 | tf_op jit(solution)/shard_map/transform/pallas_call | solution.py:200
  144.0 1.7 collective-permute-start.17
  146.1 2.6 collective-permute-start.19
  148.8 25.6 %transform.11 = (f32[8,64,128]{2,1,0:T(8,128)}, f32[8,64,128]{2,1,0:T(8,128)}, f32[8,64,128]{2,1,0:T(8,128)}, f32[8,64,128]{2,1,0:T(8,128)}, f32[8,64,128]{2,1,0...) custom-call(s32[1]{0:T(128)} %bitcast.3.rank_ref, ...), custom_call_target="tpu_custom_call" | custom-call | flops 12884901888 | bytes 37748736 | tf_op jit(solution)/shard_map/transform/pallas_call | solution.py:200
  177.1 1.7 collective-permute-start.38
  179.2 2.5 collective-permute-start.40
  181.7 3.3 collective-permute-done.36.rest_2_
  185.1 3.7 collective-permute-done.37.rest_3_
  193.3 1.7 collective-permute-start.31
  195.0 3.7 collective-permute-done.40.rest_6_
  199.6 4.4 %filter.11 = f32[64,32,128]{2,1,0:T(8,128)} custom-call(bf16[64,128]{1,0:T(8,128)(2,1)} %pad_maximum_fusion.2.bank_ref, f32[4,128,128]{2,1,0:T(8,128)} %get-tuple-element.84.rest_0_, f32[4,128,128]{2,1,0:T(8,128)} %copy-done.21, f32[4,128,128]{2,1,0:T(8,128)} %copy-done.23, f32[4,128,128]{2,1,0:T(8,128)} %copy-done.26, f32[4,128,128]{2,1,0:T(8,128)} %copy-done.28, ...), custom_call_target="tpu_custom_call" | custom-call | flops 268435456 | bytes 3145728 | tf_op jit(solution)/shard_map/filter/pallas_call | solution.py:233
  204.0 11.2 %collective-permute-done.41.rest_7_ = f32[8,64,128]{2,1,0:T(8,128)} collective-permute-done((f32[8,64,128]{2,1,0:T(8,128)}, f32[8,64,128]{2,1,0:T(8,128)}, u32[]{:S(2)}, u32[]{:S(2)}) %collective-permute-start.41) | collective-permute-done | bytes 262176 | tf_op jit(solution)/shard_map/ppermute | solution.py:264
  215.2 2.6 collective-permute-start.43
  219.0 7.4 %collective-permute-done.30.rest_3_ = f32[8,128,128]{2,1,0:T(8,128)S(1)} collective-permute-done((f32[8,128,128]{2,1,0:T(8,128)}, f32[8,128,128]{2,1,0:T(8,128)S(1)}, u32[]{:S(2)}, u32[]{:S(2)}) %collective-permute-start.30) | collective-permute-done | bytes 524320 | tf_op jit(solution)/shard_map/ppermute | solution.py:264
  226.4 1.7 collective-permute-start.33
  228.9 46.5 %collective-permute-done.32.rest_5_ = f32[8,128,128]{2,1,0:T(8,128)S(1)} collective-permute-done((f32[8,128,128]{2,1,0:T(8,128)}, f32[8,128,128]{2,1,0:T(8,128)S(1)}, u32[]{:S(2)}, u32[]{:S(2)}) %collective-permute-start.32) | collective-permute-done | bytes 524320 | tf_op jit(solution)/shard_map/ppermute | solution.py:264
  275.4 4.5 %filter.12.rest_0_ = f32[64,32,128]{2,1,0:T(8,128)} custom-call(bf16[64,128]{1,0:T(8,128)(2,1)} %pad_maximum_fusion.2.bank_ref, f32[4,128,128]{2,1,0:T(8,128)} %get-tuple-element.80.rest_0_, f32[4,128,128]{2,1,0:T(8,128)} %copy-done.13, f32[4,128,128]{2,1,0:T(8,128)} %copy-done.14, f32[4,128,128]{2,1,0:T(8,128)} %copy-done.15, f32[4,128,128]{2,1,0:T(8,128)} %copy-done.16, ...), custom_call_target="tpu_custom_call" | custom-call | flops 268435456 | bytes 3145728 | tf_op jit(solution)/shard_map/filter/pallas_call | solution.py:233
  279.9 4.4 %filter.13.rest_2_ = f32[64,32,128]{2,1,0:T(8,128)} custom-call(bf16[64,128]{1,0:T(8,128)(2,1)} %pad_maximum_fusion.2.bank_ref, f32[4,128,128]{2,1,0:T(8,128)} %get-tuple-element.84.rest_0_, f32[4,128,128]{2,1,0:T(8,128)} %copy-done.21, f32[4,128,128]{2,1,0:T(8,128)} %copy-done.23, f32[4,128,128]{2,1,0:T(8,128)} %copy-done.26, f32[4,128,128]{2,1,0:T(8,128)} %copy-done.28, ...), custom_call_target="tpu_custom_call" | custom-call | flops 268435456 | bytes 3145728 | tf_op jit(solution)/shard_map/filter/pallas_call | solution.py:233
  284.3 2.3 collective-permute-done.33.rest_6_
  287.0 10.0 %collective-permute-done.34.rest_7_ = f32[8,128,128]{2,1,0:T(8,128)} collective-permute-done((f32[8,128,128]{2,1,0:T(8,128)}, f32[8,128,128]{2,1,0:T(8,128)}, u32[]{:S(2)}, u32[]{:S(2)}) %collective-permute-start.34) | collective-permute-done | bytes 524320 | tf_op jit(solution)/shard_map/ppermute | solution.py:264
  297.1 4.5 %filter.14 = f32[64,32,128]{2,1,0:T(8,128)} custom-call(bf16[64,128]{1,0:T(8,128)(2,1)} %pad_maximum_fusion.2.bank_ref, f32[8,128,128]{2,1,0:T(8,128)} %get-tuple-element.103.rest_0_, f32[8,128,128]{2,1,0:T(8,128)} %copy-done, f32[8,128,128]{2,1,0:T(8,128)} %copy-done.1, f32[8,128,128]{2,1,0:T(8,128)} %copy-done.2, f32[8,128,128]{2,1,0:T(8,128)} %copy-done.3, ...), custom_call_target="tpu_custom_call" | custom-call | flops 268435456 | bytes 3145728 | tf_op jit(solution)/shard_map/filter/pallas_call | solution.py:233
  301.5 3.5 collective-permute-start.51
  305.3 5.0 %collective-permute-start.48 = (f32[8,64,128]{2,1,0:T(8,128)}, f32[8,64,128]{2,1,0:T(8,128)S(1)}, u32[]{:S(2)}, u32[]{:S(2)}) collective-permute-start(f32[8,64,128]{2,1,0:T(8,128)} %get-tuple-element.148), channel_id=1, source_target_pairs={{0,5},{1,4},{2,7},{3,6},{4,1},{5,0},{6,3},{7,2},{8,13},{9,12},{10,... | collective-permute-start | bytes 786440 | tf_op jit(solution)/shard_map/ppermute | solution.py:264
  311.5 20.8 %collective-permute-done.42.rest_1_ = f32[64,32,128]{2,1,0:T(8,128)} collective-permute-done((f32[64,32,128]{2,1,0:T(8,128)}, f32[64,32,128]{2,1,0:T(8,128)}, u32[]{:S(2)}, u32[]{:S(2)}) %collective-permute-start.42) | collective-permute-done | bytes 1048608 | tf_op jit(solution)/shard_map/ppermute | solution.py:264
  333.8 4.5 %filter.15.rest_1_ = f32[64,32,128]{2,1,0:T(8,128)} custom-call(bf16[64,128]{1,0:T(8,128)(2,1)} %pad_maximum_fusion.2.bank_ref, f32[8,128,128]{2,1,0:T(8,128)} %get-tuple-element.103.rest_0_, f32[8,128,128]{2,1,0:T(8,128)} %copy-done, f32[8,128,128]{2,1,0:T(8,128)} %copy-done.1, f32[8,128,128]{2,1,0:T(8,128)} %copy-done.2, f32[8,128,128]{2,1,0:T(8,128)} %copy-done.3, ...), custom_call_target="tpu_custom_call" | custom-call | flops 268435456 | bytes 3145728 | tf_op jit(solution)/shard_map/filter/pallas_call | solution.py:233
  338.2 2.7 filter.16
  341.0 2.7 filter.17.rest_3_
  343.7 3.2 energy.2.rest_0_
  346.9 2.8 collective-permute-start.52
  349.7 9.0 %collective-permute-done.50.rest_7_ = f32[8,64,128]{2,1,0:T(8,128)S(1)} collective-permute-done((f32[8,64,128]{2,1,0:T(8,128)}, f32[8,64,128]{2,1,0:T(8,128)S(1)}, u32[]{:S(2)}, u32[]{:S(2)}) %collective-permute-start.50) | collective-permute-done | bytes 262176 | tf_op jit(solution)/shard_map/ppermute | solution.py:264
  359.4 2.7 filter.18
  362.2 2.7 filter.19.rest_5_
  364.9 23.5 %collective-permute-done.52.rest_4_ = f32[32,32,128]{2,1,0:T(8,128)S(1)} collective-permute-done((f32[32,32,128]{2,1,0:T(8,128)}, f32[32,32,128]{2,1,0:T(8,128)S(1)}, u32[]{:S(2)}, u32[]{:S(2)}) %collective-permute-start.52) | collective-permute-done | bytes 524320 | tf_op jit(solution)/shard_map/ppermute | solution.py:264
  388.4 10.3 %collective-permute-done.53.rest_6_ = f32[32,32,128]{2,1,0:T(8,128)S(1)} collective-permute-done((f32[32,32,128]{2,1,0:T(8,128)}, f32[32,32,128]{2,1,0:T(8,128)S(1)}, u32[]{:S(2)}, u32[]{:S(2)}) %collective-permute-start.53) | collective-permute-done | bytes 524320 | tf_op jit(solution)/shard_map/ppermute | solution.py:264
  400.5 3.2 energy.3
  (200 shorter events, 37.0 us)
Async XLA Ops:
  31.0 35.2 %collective-permute-start.10 = (f32[4,128,128]{2,1,0:T(8,128)}, f32[4,128,128]{2,1,0:T(8,128)S(1)}, u32[]{:S(2)}, u32[]{:S(2)}) collective-permute-start(f32[4,128,128]{2,1,0:T(8,128)} %get-tuple-element.98), channel_id=1, source_target_pairs={{0,4},{1,5},{2,6},{3,7},{4,0},{5,1},{6,2},{7,3},{8,12},{9,13},{10,... | collective-permute-start | bytes 786440 | tf_op jit(solution)/shard_map/ppermute | solution.py:264
  34.2 33.6 %collective-permute-start.11 = (f32[4,128,128]{2,1,0:T(8,128)}, f32[4,128,128]{2,1,0:T(8,128)S(1)}, u32[]{:S(2)}, u32[]{:S(2)}) collective-permute-start(f32[4,128,128]{2,1,0:T(8,128)} %get-tuple-element.99), channel_id=1, source_target_pairs={{0,5},{1,4},{2,7},{3,6},{4,1},{5,0},{6,3},{7,2},{8,13},{9,12},{10,... | collective-permute-start | bytes 786440 | tf_op jit(solution)/shard_map/ppermute | solution.py:264
  34.2 33.7 %collective-permute-start.12 = (f32[4,128,128]{2,1,0:T(8,128)}, f32[4,128,128]{2,1,0:T(8,128)S(1)}, u32[]{:S(2)}, u32[]{:S(2)}) collective-permute-start(f32[4,128,128]{2,1,0:T(8,128)} %get-tuple-element.100), channel_id=1, source_target_pairs={{0,6},{1,7},{2,4},{3,5},{4,2},{5,3},{6,0},{7,1},{8,14},{9,15},{10,... | collective-permute-start | bytes 786440 | tf_op jit(solution)/shard_map/ppermute | solution.py:264
  36.3 32.5 %collective-permute-start.13 = (f32[4,128,128]{2,1,0:T(8,128)}, f32[4,128,128]{2,1,0:T(8,128)S(1)}, u32[]{:S(2)}, u32[]{:S(2)}) collective-permute-start(f32[4,128,128]{2,1,0:T(8,128)} %get-tuple-element.101), channel_id=1, source_target_pairs={{0,7},{1,6},{2,5},{3,4},{4,3},{5,2},{6,1},{7,0},{8,15},{9,14},{10,... | collective-permute-start | bytes 786440 | tf_op jit(solution)/shard_map/ppermute | solution.py:264
  36.8 33.5 %collective-permute-start.7 = (f32[4,128,128]{2,1,0:T(8,128)}, f32[4,128,128]{2,1,0:T(8,128)S(1)}, u32[]{:S(2)}, u32[]{:S(2)}) collective-permute-start(f32[4,128,128]{2,1,0:T(8,128)} %get-tuple-element.95), channel_id=1, source_target_pairs={{0,1},{1,0},{2,3},{3,2},{4,5},{5,4},{6,7},{7,6},{8,9},{9,8},{10,11... | collective-permute-start | bytes 786440 | tf_op jit(solution)/shard_map/ppermute | solution.py:264
  67.8 12.3 %collective-permute-start.9 = (f32[4,128,128]{2,1,0:T(8,128)S(1)}, f32[4,128,128]{2,1,0:T(8,128)S(1)}, u32[]{:S(2)}, u32[]{:S(2)}) collective-permute-start(f32[4,128,128]{2,1,0:T(8,128)S(1)} %copy-done.48), channel_id=1, source_target_pairs={{0,3},{1,2},{2,1},{3,0},{4,7},{5,6},{6,5},{7,4},{8,11},{9,10},{10,... | collective-permute-start | bytes 786440 | tf_op jit(solution)/shard_map/ppermute | solution.py:264
  67.9 14.3 %collective-permute-start = (f32[4,128,128]{2,1,0:T(8,128)S(1)}, f32[4,128,128]{2,1,0:T(8,128)S(1)}, u32[]{:S(2)}, u32[]{:S(2)}) collective-permute-start(f32[4,128,128]{2,1,0:T(8,128)S(1)} %copy-done.47), channel_id=1, source_target_pairs={{0,1},{1,0},{2,3},{3,2},{4,5},{5,4},{6,7},{7,6},{8,9},{9,8},{10,11... | collective-permute-start | bytes 786440 | tf_op jit(solution)/shard_map/ppermute | solution.py:264
  68.8 17.9 %collective-permute-start.1 = (f32[4,128,128]{2,1,0:T(8,128)}, f32[4,128,128]{2,1,0:T(8,128)S(1)}, u32[]{:S(2)}, u32[]{:S(2)}) collective-permute-start(f32[4,128,128]{2,1,0:T(8,128)} %get-tuple-element.89), channel_id=1, source_target_pairs={{0,2},{1,3},{2,0},{3,1},{4,6},{5,7},{6,4},{7,5},{8,10},{9,11},{10,... | collective-permute-start | bytes 786440 | tf_op jit(solution)/shard_map/ppermute | solution.py:264
  70.3 31.7 %collective-permute-start.2 = (f32[4,128,128]{2,1,0:T(8,128)}, f32[4,128,128]{2,1,0:T(8,128)S(1)}, u32[]{:S(2)}, u32[]{:S(2)}) collective-permute-start(f32[4,128,128]{2,1,0:T(8,128)} %get-tuple-element.90), channel_id=1, source_target_pairs={{0,3},{1,2},{2,1},{3,0},{4,7},{5,6},{6,5},{7,4},{8,11},{9,10},{10,... | collective-permute-start | bytes 786440 | tf_op jit(solution)/shard_map/ppermute | solution.py:264
  75.5 27.1 %collective-permute-start.3 = (f32[4,128,128]{2,1,0:T(8,128)}, f32[4,128,128]{2,1,0:T(8,128)S(1)}, u32[]{:S(2)}, u32[]{:S(2)}) collective-permute-start(f32[4,128,128]{2,1,0:T(8,128)} %get-tuple-element.91), channel_id=1, source_target_pairs={{0,4},{1,5},{2,6},{3,7},{4,0},{5,1},{6,2},{7,3},{8,12},{9,13},{10,... | collective-permute-start | bytes 786440 | tf_op jit(solution)/shard_map/ppermute | solution.py:264
  80.1 24.1 %collective-permute-start.4 = (f32[4,128,128]{2,1,0:T(8,128)}, f32[4,128,128]{2,1,0:T(8,128)S(1)}, u32[]{:S(2)}, u32[]{:S(2)}) collective-permute-start(f32[4,128,128]{2,1,0:T(8,128)} %get-tuple-element.92), channel_id=1, source_target_pairs={{0,5},{1,4},{2,7},{3,6},{4,1},{5,0},{6,3},{7,2},{8,13},{9,12},{10,... | collective-permute-start | bytes 786440 | tf_op jit(solution)/shard_map/ppermute | solution.py:264
  82.2 22.1 %collective-permute-start.5 = (f32[4,128,128]{2,1,0:T(8,128)}, f32[4,128,128]{2,1,0:T(8,128)S(1)}, u32[]{:S(2)}, u32[]{:S(2)}) collective-permute-start(f32[4,128,128]{2,1,0:T(8,128)} %get-tuple-element.93), channel_id=1, source_target_pairs={{0,6},{1,7},{2,4},{3,5},{4,2},{5,3},{6,0},{7,1},{8,14},{9,15},{10,... | collective-permute-start | bytes 786440 | tf_op jit(solution)/shard_map/ppermute | solution.py:264
  86.7 20.1 %collective-permute-start.6 = (f32[4,128,128]{2,1,0:T(8,128)}, f32[4,128,128]{2,1,0:T(8,128)}, u32[]{:S(2)}, u32[]{:S(2)}) collective-permute-start(f32[4,128,128]{2,1,0:T(8,128)} %get-tuple-element.94), channel_id=1, source_target_pairs={{0,7},{1,6},{2,5},{3,4},{4,3},{5,2},{6,1},{7,0},{8,15},{9,14},{10,... | collective-permute-start | bytes 786440 | tf_op jit(solution)/shard_map/ppermute | solution.py:264
  104.2 11.7 %collective-permute-start.23 = (f32[4,128,128]{2,1,0:T(8,128)}, f32[4,128,128]{2,1,0:T(8,128)}, u32[]{:S(2)}, u32[]{:S(2)}) collective-permute-start(f32[4,128,128]{2,1,0:T(8,128)} %get-tuple-element.116), channel_id=1, source_target_pairs={{0,3},{1,2},{2,1},{3,0},{4,7},{5,6},{6,5},{7,4},{8,11},{9,10},{10,... | collective-permute-start | bytes 786440 | tf_op jit(solution)/shard_map/ppermute | solution.py:264
  104.3 12.6 %collective-permute-start.24 = (f32[4,128,128]{2,1,0:T(8,128)}, f32[4,128,128]{2,1,0:T(8,128)}, u32[]{:S(2)}, u32[]{:S(2)}) collective-permute-start(f32[4,128,128]{2,1,0:T(8,128)} %get-tuple-element.117), channel_id=1, source_target_pairs={{0,4},{1,5},{2,6},{3,7},{4,0},{5,1},{6,2},{7,3},{8,12},{9,13},{10,... | collective-permute-start | bytes 786440 | tf_op jit(solution)/shard_map/ppermute | solution.py:264
  106.8 37.0 %collective-permute-start.25 = (f32[4,128,128]{2,1,0:T(8,128)}, f32[4,128,128]{2,1,0:T(8,128)}, u32[]{:S(2)}, u32[]{:S(2)}) collective-permute-start(f32[4,128,128]{2,1,0:T(8,128)} %get-tuple-element.118), channel_id=1, source_target_pairs={{0,5},{1,4},{2,7},{3,6},{4,1},{5,0},{6,3},{7,2},{8,13},{9,12},{10,... | collective-permute-start | bytes 786440 | tf_op jit(solution)/shard_map/ppermute | solution.py:264
  111.6 32.4 %collective-permute-start.26 = (f32[4,128,128]{2,1,0:T(8,128)}, f32[4,128,128]{2,1,0:T(8,128)S(1)}, u32[]{:S(2)}, u32[]{:S(2)}) collective-permute-start(f32[4,128,128]{2,1,0:T(8,128)} %get-tuple-element.119), channel_id=1, source_target_pairs={{0,6},{1,7},{2,4},{3,5},{4,2},{5,3},{6,0},{7,1},{8,14},{9,15},{10,... | collective-permute-start | bytes 786440 | tf_op jit(solution)/shard_map/ppermute | solution.py:264
  114.3 31.4 %collective-permute-start.27 = (f32[4,128,128]{2,1,0:T(8,128)}, f32[4,128,128]{2,1,0:T(8,128)S(1)}, u32[]{:S(2)}, u32[]{:S(2)}) collective-permute-start(f32[4,128,128]{2,1,0:T(8,128)} %get-tuple-element.120), channel_id=1, source_target_pairs={{0,7},{1,6},{2,5},{3,4},{4,3},{5,2},{6,1},{7,0},{8,15},{9,14},{10,... | collective-permute-start | bytes 786440 | tf_op jit(solution)/shard_map/ppermute | solution.py:264
  116.0 30.1 %collective-permute-start.14 = (f32[4,128,128]{2,1,0:T(8,128)}, f32[4,128,128]{2,1,0:T(8,128)S(1)}, u32[]{:S(2)}, u32[]{:S(2)}) collective-permute-start(f32[4,128,128]{2,1,0:T(8,128)} %get-tuple-element.107), channel_id=1, source_target_pairs={{0,1},{1,0},{2,3},{3,2},{4,5},{5,4},{6,7},{7,6},{8,9},{9,8},{10,11... | collective-permute-start | bytes 786440 | tf_op jit(solution)/shard_map/ppermute | solution.py:264
  116.9 31.8 %collective-permute-start.15 = (f32[4,128,128]{2,1,0:T(8,128)}, f32[4,128,128]{2,1,0:T(8,128)S(1)}, u32[]{:S(2)}, u32[]{:S(2)}) collective-permute-start(f32[4,128,128]{2,1,0:T(8,128)} %get-tuple-element.108), channel_id=1, source_target_pairs={{0,2},{1,3},{2,0},{3,1},{4,6},{5,7},{6,4},{7,5},{8,10},{9,11},{10,... | collective-permute-start | bytes 786440 | tf_op jit(solution)/shard_map/ppermute | solution.py:264
  143.9 30.6 %collective-permute-start.16 = (f32[4,128,128]{2,1,0:T(8,128)}, f32[4,128,128]{2,1,0:T(8,128)S(1)}, u32[]{:S(2)}, u32[]{:S(2)}) collective-permute-start(f32[4,128,128]{2,1,0:T(8,128)} %get-tuple-element.109), channel_id=1, source_target_pairs={{0,3},{1,2},{2,1},{3,0},{4,7},{5,6},{6,5},{7,4},{8,11},{9,10},{10,... | collective-permute-start | bytes 786440 | tf_op jit(solution)/shard_map/ppermute | solution.py:264
  144.0 31.6 %collective-permute-start.17 = (f32[4,128,128]{2,1,0:T(8,128)S(1)}, f32[4,128,128]{2,1,0:T(8,128)S(1)}, u32[]{:S(2)}, u32[]{:S(2)}) collective-permute-start(f32[4,128,128]{2,1,0:T(8,128)S(1)} %copy-done.46), channel_id=1, source_target_pairs={{0,4},{1,5},{2,6},{3,7},{4,0},{5,1},{6,2},{7,3},{8,12},{9,13},{10,... | collective-permute-start | bytes 786440 | tf_op jit(solution)/shard_map/ppermute | solution.py:264
  145.7 31.4 %collective-permute-start.18 = (f32[4,128,128]{2,1,0:T(8,128)S(1)}, f32[4,128,128]{2,1,0:T(8,128)S(1)}, u32[]{:S(2)}, u32[]{:S(2)}) collective-permute-start(f32[4,128,128]{2,1,0:T(8,128)S(1)} %copy-done.45), channel_id=1, source_target_pairs={{0,5},{1,4},{2,7},{3,6},{4,1},{5,0},{6,3},{7,2},{8,13},{9,12},{10,... | collective-permute-start | bytes 786440 | tf_op jit(solution)/shard_map/ppermute | solution.py:264
  146.1 31.0 %collective-permute-start.19 = (f32[4,128,128]{2,1,0:T(8,128)S(1)}, f32[4,128,128]{2,1,0:T(8,128)S(1)}, u32[]{:S(2)}, u32[]{:S(2)}) collective-permute-start(f32[4,128,128]{2,1,0:T(8,128)S(1)} %copy-done.44), channel_id=1, source_target_pairs={{0,6},{1,7},{2,4},{3,5},{4,2},{5,3},{6,0},{7,1},{8,14},{9,15},{10,... | collective-permute-start | bytes 786440 | tf_op jit(solution)/shard_map/ppermute | solution.py:264
  148.7 30.1 %collective-permute-start.20 = (f32[4,128,128]{2,1,0:T(8,128)S(1)}, f32[4,128,128]{2,1,0:T(8,128)S(1)}, u32[]{:S(2)}, u32[]{:S(2)}) collective-permute-start(f32[4,128,128]{2,1,0:T(8,128)S(1)} %copy-done.43), channel_id=1, source_target_pairs={{0,7},{1,6},{2,5},{3,4},{4,3},{5,2},{6,1},{7,0},{8,15},{9,14},{10,... | collective-permute-start | bytes 786440 | tf_op jit(solution)/shard_map/ppermute | solution.py:264
  177.1 11.7 %collective-permute-start.37 = (f32[8,64,128]{2,1,0:T(8,128)}, f32[8,64,128]{2,1,0:T(8,128)S(1)}, u32[]{:S(2)}, u32[]{:S(2)}) collective-permute-start(f32[8,64,128]{2,1,0:T(8,128)} %get-tuple-element.135), channel_id=1, source_target_pairs={{0,3},{1,2},{2,1},{3,0},{4,7},{5,6},{6,5},{7,4},{8,11},{9,10},{10,... | collective-permute-start | bytes 786440 | tf_op jit(solution)/shard_map/ppermute | solution.py:264
  177.1 13.9 %collective-permute-start.38 = (f32[8,64,128]{2,1,0:T(8,128)}, f32[8,64,128]{2,1,0:T(8,128)S(1)}, u32[]{:S(2)}, u32[]{:S(2)}) collective-permute-start(f32[8,64,128]{2,1,0:T(8,128)} %get-tuple-element.136), channel_id=1, source_target_pairs={{0,4},{1,5},{2,6},{3,7},{4,0},{5,1},{6,2},{7,3},{8,12},{9,13},{10,... | collective-permute-start | bytes 786440 | tf_op jit(solution)/shard_map/ppermute | solution.py:264
  178.8 13.8 %collective-permute-start.39 = (f32[8,64,128]{2,1,0:T(8,128)}, f32[8,64,128]{2,1,0:T(8,128)S(1)}, u32[]{:S(2)}, u32[]{:S(2)}) collective-permute-start(f32[8,64,128]{2,1,0:T(8,128)} %get-tuple-element.137), channel_id=1, source_target_pairs={{0,5},{1,4},{2,7},{3,6},{4,1},{5,0},{6,3},{7,2},{8,13},{9,12},{10,... | collective-permute-start | bytes 786440 | tf_op jit(solution)/shard_map/ppermute | solution.py:264
  179.2 19.6 %collective-permute-start.40 = (f32[8,64,128]{2,1,0:T(8,128)}, f32[8,64,128]{2,1,0:T(8,128)}, u32[]{:S(2)}, u32[]{:S(2)}) collective-permute-start(f32[8,64,128]{2,1,0:T(8,128)} %get-tuple-element.138), channel_id=1, source_target_pairs={{0,6},{1,7},{2,4},{3,5},{4,2},{5,3},{6,0},{7,1},{8,14},{9,15},{10,... | collective-permute-start | bytes 786440 | tf_op jit(solution)/shard_map/ppermute | solution.py:264
  185.0 32.8 %collective-permute-start.28 = (f32[8,128,128]{2,1,0:T(8,128)}, f32[8,128,128]{2,1,0:T(8,128)S(1)}, u32[]{:S(2)}, u32[]{:S(2)}) collective-permute-start(f32[8,128,128]{2,1,0:T(8,128)} %get-tuple-element.124), channel_id=1, source_target_pairs={{0,1},{1,0},{2,3},{3,2},{4,5},{5,4},{6,7},{7,6},{8,9},{9,8},{10,11... | collective-permute-start | bytes 1572872 | tf_op jit(solution)/shard_map/ppermute | solution.py:264
  189.5 28.6 %collective-permute-start.29 = (f32[8,128,128]{2,1,0:T(8,128)}, f32[8,128,128]{2,1,0:T(8,128)S(1)}, u32[]{:S(2)}, u32[]{:S(2)}) collective-permute-start(f32[8,128,128]{2,1,0:T(8,128)} %get-tuple-element.125), channel_id=1, source_target_pairs={{0,2},{1,3},{2,0},{3,1},{4,6},{5,7},{6,4},{7,5},{8,10},{9,11},{10,... | collective-permute-start | bytes 1572872 | tf_op jit(solution)/shard_map/ppermute | solution.py:264
  191.7 34.7 %collective-permute-start.30 = (f32[8,128,128]{2,1,0:T(8,128)}, f32[8,128,128]{2,1,0:T(8,128)S(1)}, u32[]{:S(2)}, u32[]{:S(2)}) collective-permute-start(f32[8,128,128]{2,1,0:T(8,128)} %get-tuple-element.126), channel_id=1, source_target_pairs={{0,3},{1,2},{2,1},{3,0},{4,7},{5,6},{6,5},{7,4},{8,11},{9,10},{10,... | collective-permute-start | bytes 1572872 | tf_op jit(solution)/shard_map/ppermute | solution.py:264
  193.3 34.8 %collective-permute-start.31 = (f32[8,128,128]{2,1,0:T(8,128)}, f32[8,128,128]{2,1,0:T(8,128)S(1)}, u32[]{:S(2)}, u32[]{:S(2)}) collective-permute-start(f32[8,128,128]{2,1,0:T(8,128)} %get-tuple-element.127), channel_id=1, source_target_pairs={{0,4},{1,5},{2,6},{3,7},{4,0},{5,1},{6,2},{7,3},{8,12},{9,13},{10,... | collective-permute-start | bytes 1572872 | tf_op jit(solution)/shard_map/ppermute | solution.py:264
  198.7 16.5 %collective-permute-start.41 = (f32[8,64,128]{2,1,0:T(8,128)}, f32[8,64,128]{2,1,0:T(8,128)}, u32[]{:S(2)}, u32[]{:S(2)}) collective-permute-start(f32[8,64,128]{2,1,0:T(8,128)} %get-tuple-element.139), channel_id=1, source_target_pairs={{0,7},{1,6},{2,5},{3,4},{4,3},{5,2},{6,1},{7,0},{8,15},{9,14},{10,... | collective-permute-start | bytes 786440 | tf_op jit(solution)/shard_map/ppermute | solution.py:264
  215.2 95.1 %collective-permute-start.43 = (f32[64,32,128]{2,1,0:T(8,128)}, f32[64,32,128]{2,1,0:T(8,128)}, u32[]{:S(2)}, u32[]{:S(2)}) collective-permute-start(f32[64,32,128]{2,1,0:T(8,128)} %filter.11), channel_id=1, source_target_pairs={{0,8},{1,9},{2,10},{3,11},{4,12},{5,13},{6,14},{7,15},{8,0},{9,1},... | collective-permute-start | bytes 3145736 | tf_op jit(solution)/shard_map/ppermute | solution.py:264
  217.8 114.5 %collective-permute-start.42 = (f32[64,32,128]{2,1,0:T(8,128)}, f32[64,32,128]{2,1,0:T(8,128)}, u32[]{:S(2)}, u32[]{:S(2)}) collective-permute-start(f32[64,32,128]{2,1,0:T(8,128)} %filter.10), channel_id=1, source_target_pairs={{0,8},{1,9},{2,10},{3,11},{4,12},{5,13},{6,14},{7,15},{8,0},{9,1},... | collective-permute-start | bytes 3145736 | tf_op jit(solution)/shard_map/ppermute | solution.py:264
  218.1 57.3 %collective-permute-start.32 = (f32[8,128,128]{2,1,0:T(8,128)}, f32[8,128,128]{2,1,0:T(8,128)S(1)}, u32[]{:S(2)}, u32[]{:S(2)}) collective-permute-start(f32[8,128,128]{2,1,0:T(8,128)} %get-tuple-element.128), channel_id=1, source_target_pairs={{0,5},{1,4},{2,7},{3,6},{4,1},{5,0},{6,3},{7,2},{8,13},{9,12},{10,... | collective-permute-start | bytes 1572872 | tf_op jit(solution)/shard_map/ppermute | solution.py:264
  226.4 60.2 %collective-permute-start.33 = (f32[8,128,128]{2,1,0:T(8,128)}, f32[8,128,128]{2,1,0:T(8,128)S(1)}, u32[]{:S(2)}, u32[]{:S(2)}) collective-permute-start(f32[8,128,128]{2,1,0:T(8,128)} %get-tuple-element.129), channel_id=1, source_target_pairs={{0,6},{1,7},{2,4},{3,5},{4,2},{5,3},{6,0},{7,1},{8,14},{9,15},{10,... | collective-permute-start | bytes 1572872 | tf_op jit(solution)/shard_map/ppermute | solution.py:264
  228.1 68.9 %collective-permute-start.34 = (f32[8,128,128]{2,1,0:T(8,128)}, f32[8,128,128]{2,1,0:T(8,128)}, u32[]{:S(2)}, u32[]{:S(2)}) collective-permute-start(f32[8,128,128]{2,1,0:T(8,128)} %get-tuple-element.130), channel_id=1, source_target_pairs={{0,7},{1,6},{2,5},{3,4},{4,3},{5,2},{6,1},{7,0},{8,15},{9,14},{10,... | collective-permute-start | bytes 1572872 | tf_op jit(solution)/shard_map/ppermute | solution.py:264
  275.4 26.1 %collective-permute-start.44 = (f32[8,64,128]{2,1,0:T(8,128)}, f32[8,64,128]{2,1,0:T(8,128)S(1)}, u32[]{:S(2)}, u32[]{:S(2)}) collective-permute-start(f32[8,64,128]{2,1,0:T(8,128)} %get-tuple-element.144), channel_id=1, source_target_pairs={{0,1},{1,0},{2,3},{3,2},{4,5},{5,4},{6,7},{7,6},{8,9},{9,8},{10,11... | collective-permute-start | bytes 786440 | tf_op jit(solution)/shard_map/ppermute | solution.py:264
  286.6 18.4 %collective-permute-start.45 = (f32[8,64,128]{2,1,0:T(8,128)}, f32[8,64,128]{2,1,0:T(8,128)}, u32[]{:S(2)}, u32[]{:S(2)}) collective-permute-start(f32[8,64,128]{2,1,0:T(8,128)} %get-tuple-element.145), channel_id=1, source_target_pairs={{0,2},{1,3},{2,0},{3,1},{4,6},{5,7},{6,4},{7,5},{8,10},{9,11},{10,... | collective-permute-start | bytes 786440 | tf_op jit(solution)/shard_map/ppermute | solution.py:264
  301.5 97.2 %collective-permute-start.51 = (f32[64,32,128]{2,1,0:T(8,128)}, f32[64,32,128]{2,1,0:T(8,128)S(1)}, u32[]{:S(2)}, u32[]{:S(2)}) collective-permute-start(f32[64,32,128]{2,1,0:T(8,128)} %filter.14), channel_id=1, source_target_pairs={{0,8},{1,9},{2,10},{3,11},{4,12},{5,13},{6,14},{7,15},{8,0},{9,1},... | collective-permute-start | bytes 3145736 | tf_op jit(solution)/shard_map/ppermute | solution.py:264
  305.0 41.9 %collective-permute-start.47 = (f32[8,64,128]{2,1,0:T(8,128)}, f32[8,64,128]{2,1,0:T(8,128)S(1)}, u32[]{:S(2)}, u32[]{:S(2)}) collective-permute-start(f32[8,64,128]{2,1,0:T(8,128)} %get-tuple-element.147), channel_id=1, source_target_pairs={{0,4},{1,5},{2,6},{3,7},{4,0},{5,1},{6,2},{7,3},{8,12},{9,13},{10,... | collective-permute-start | bytes 786440 | tf_op jit(solution)/shard_map/ppermute | solution.py:264
  305.3 44.4 %collective-permute-start.48 = (f32[8,64,128]{2,1,0:T(8,128)}, f32[8,64,128]{2,1,0:T(8,128)S(1)}, u32[]{:S(2)}, u32[]{:S(2)}) collective-permute-start(f32[8,64,128]{2,1,0:T(8,128)} %get-tuple-element.148), channel_id=1, source_target_pairs={{0,5},{1,4},{2,7},{3,6},{4,1},{5,0},{6,3},{7,2},{8,13},{9,12},{10,... | collective-permute-start | bytes 786440 | tf_op jit(solution)/shard_map/ppermute | solution.py:264
  310.3 39.4 %collective-permute-start.49 = (f32[8,64,128]{2,1,0:T(8,128)}, f32[8,64,128]{2,1,0:T(8,128)S(1)}, u32[]{:S(2)}, u32[]{:S(2)}) collective-permute-start(f32[8,64,128]{2,1,0:T(8,128)} %get-tuple-element.149), channel_id=1, source_target_pairs={{0,6},{1,7},{2,4},{3,5},{4,2},{5,3},{6,0},{7,1},{8,14},{9,15},{10,... | collective-permute-start | bytes 786440 | tf_op jit(solution)/shard_map/ppermute | solution.py:264
  332.3 26.4 %collective-permute-start.50 = (f32[8,64,128]{2,1,0:T(8,128)}, f32[8,64,128]{2,1,0:T(8,128)S(1)}, u32[]{:S(2)}, u32[]{:S(2)}) collective-permute-start(f32[8,64,128]{2,1,0:T(8,128)} %get-tuple-element.150), channel_id=1, source_target_pairs={{0,7},{1,6},{2,5},{3,4},{4,3},{5,2},{6,1},{7,0},{8,15},{9,14},{10,... | collective-permute-start | bytes 786440 | tf_op jit(solution)/shard_map/ppermute | solution.py:264
  346.9 41.5 %collective-permute-start.52 = (f32[32,32,128]{2,1,0:T(8,128)}, f32[32,32,128]{2,1,0:T(8,128)S(1)}, u32[]{:S(2)}, u32[]{:S(2)}) collective-permute-start(f32[32,32,128]{2,1,0:T(8,128)} %filter.16), channel_id=1, source_target_pairs={{0,8},{1,9},{2,10},{3,11},{4,12},{5,13},{6,14},{7,15},{8,0},{9,1},... | collective-permute-start | bytes 1572872 | tf_op jit(solution)/shard_map/ppermute | solution.py:264
  362.1 36.6 %collective-permute-start.53 = (f32[32,32,128]{2,1,0:T(8,128)}, f32[32,32,128]{2,1,0:T(8,128)S(1)}, u32[]{:S(2)}, u32[]{:S(2)}) collective-permute-start(f32[32,32,128]{2,1,0:T(8,128)} %filter.18), channel_id=1, source_target_pairs={{0,8},{1,9},{2,10},{3,11},{4,12},{5,13},{6,14},{7,15},{8,0},{9,1},... | collective-permute-start | bytes 1572872 | tf_op jit(solution)/shard_map/ppermute | solution.py:264
  (56 other events, 1414.6 us)

commit v2 on v1

v2 whole, which is shorter than its diff:
```python
import functools
import math

import jax
import jax.numpy as jnp
import numpy as np
from jax import lax
from jax.experimental import pallas as pl
from jax.experimental.pallas import tpu as pltpu
from jax.sharding import PartitionSpec as P

KY = 256
TAPS = 31
BANDS = 8
OUTS = 4
BINS = 128
LANES = 2 * BINS


def split_bf16(values):
    high = values.astype(jnp.bfloat16)
    low = (values - high.astype(jnp.float32)).astype(jnp.bfloat16)
    return high, low


def split_exact(values):
    high = lax.reduce_precision(values, 8, 7)
    return high.astype(jnp.bfloat16), (values - high).astype(jnp.bfloat16)


def split_host(values):
    values = values.astype(np.float32)
    high = values.astype(jnp.bfloat16)
    low = (values - high.astype(np.float32)).astype(jnp.bfloat16)
    return high, low


def times_i(values):
    return jnp.concatenate([-values[:, BINS:], values[:, :BINS]], 1)


def dot32(left, right):
    return jnp.dot(left, right, preferred_element_type=jnp.float32)


def transform_kernel(parts, share, groups, rank_ref, p_ref, factor_ref, mh_ref, ml_ref, twc_ref, tws_ref, *rest):
    outs, (th_ref, tl_ref, g_ref, f_ref) = rest[:-4], rest[-4:]
    half = groups // 2
    radix = f_ref.shape[0]
    rows = p_ref.shape[1]
    span = rows // radix
    block = 256
    fine = factor_ref.shape[1]

    @pl.when(pl.program_id(0) == 0)
    def _():
        for a in range(p_ref.shape[2] // fine):
            at = slice(a, a + 1)
            both = factor_ref[0, at, :] * factor_ref[2] - factor_ref[1, at, :] * factor_ref[3]
            high, low = split_bf16(both)
            th_ref[a * fine : (a + 1) * fine, :] = high
            tl_ref[a * fine : (a + 1) * fine, :] = low

    @pl.loop(0, rows // block)
    def _(r):
        at = pl.ds(pl.multiple_of(r * block, block), block)
        high, low = split_bf16(p_ref[0, at, :])
        g_ref[at, :] = dot32(high, th_ref[...]) + dot32(high, tl_ref[...]) + dot32(low, th_ref[...])

    fields = [g_ref[r * span : (r + 1) * span, :] for r in range(radix)]
    if radix == 4:
        a, b = fields[0] + fields[2], fields[0] - fields[2]
        c, d = fields[1] + fields[3], times_i(fields[1] - fields[3])
        fields = [a + c, b - d, a - c, b + d]
    elif radix == 2:
        fields = [fields[0] + fields[1], fields[0] - fields[1]]
    for s, field in enumerate(fields):
        if s:
            cosine = jnp.concatenate([twc_ref[s], twc_ref[s]], 1)
            sine = jnp.concatenate([tws_ref[s], tws_ref[s]], 1)
            field = cosine * field + sine * times_i(field)
        high, low = split_bf16(jnp.concatenate([field, times_i(field)], 0))
        f_ref[s] = dot32(mh_ref[...], high) + dot32(mh_ref[...], low) + dot32(ml_ref[...], high)
    for q, part in enumerate(parts):
        for k in range(half):
            for h in range(2):
                at = pl.ds(pl.multiple_of((rank_ref[0] ^ (k + h * half)) * share, share), share)
                for n, s in enumerate(part):
                    first = (h * len(part) + n) * share
                    outs[q * half + k][0, first : first + share, :] = f_ref[s, at, :]


def filter_kernel(places, bank_ref, *rest):
    pieces, (out, re_ref, im_ref) = rest[:-3], rest[-3:]
    signals, rows = out.shape[1], out.shape[0]
    snaps = re_ref.shape[0] // rows
    for place, piece in zip(places, pieces):
        for t in range(piece.shape[0]):
            first = (place + t) * rows
            re_ref[first : first + rows, :] = piece[t, :, :BINS]
            im_ref[first : first + rows, :] = piece[t, :, BINS:]
    for r in range(rows):
        at = pl.ds(r, snaps, stride=rows)
        re, im = re_ref[at, :], im_ref[at, :]
        high, low = split_bf16(
            jnp.concatenate([jnp.concatenate([re, im], 1), jnp.concatenate([-im, re], 1)], 0)
        )
        both = dot32(bank_ref[...], high)
        out[r] = both[:signals] + both[signals:] + dot32(bank_ref[:signals, :], low)


def energy_kernel(parts, share, radix, held, scale_ref, *rest):
    fields, out, e_ref = rest[held:-2], rest[-2], rest[-1]
    rows = out.shape[1]
    for q, part in enumerate(parts):
        own, other = fields[2 * q], fields[2 * q + 1]
        for n, s in enumerate(part):
            for i in range(share):
                field = own[n * share + i] + other[n * share + i]
                power = field * field
                power = power[:, :BINS] + power[:, BINS:]
                total = power[:BANDS]
                for j in range(1, OUTS):
                    total = total + power[j * BANDS : (j + 1) * BANDS]
                x = i * radix + s
                e_ref[x * BANDS : (x + 1) * BANDS, :] = scale_ref[0] * total
    for b in range(BANDS):
        out[b, :, :] = e_ref[pl.ds(b, rows, stride=BANDS), :]


def filter_bank(centres, strides, snaps, times):
    tap_index = jnp.arange(TAPS, dtype=jnp.int32)
    window = 0.5 - 0.5 * jnp.cos(2.0 * math.pi * (tap_index.astype(jnp.float32) + 1.0) / (TAPS + 1))
    phase_index = centres[:, None] * tap_index[None, :] % snaps
    phase_angle = -2.0 * math.pi * phase_index.astype(jnp.float32) / snaps
    tap_real = window[None, :] * jnp.cos(phase_angle)
    tap_imag = window[None, :] * jnp.sin(phase_angle)
    outputs = jnp.arange(OUTS, dtype=jnp.int32)
    source = (outputs[:, None, None] * strides[None, :, None] + tap_index[None, None, :]) % snaps
    chosen = source[..., None] == times
    bank_real = jnp.sum(jnp.where(chosen, tap_real[None, :, :, None], 0.0), axis=2)
    bank_imag = jnp.sum(jnp.where(chosen, tap_imag[None, :, :, None], 0.0), axis=2)
    signals = BANDS * OUTS
    bank = jnp.concatenate(
        [bank_real.reshape(signals, -1), bank_imag.reshape(signals, -1)], axis=1
    )
    return jnp.concatenate(split_exact(bank), axis=0), jnp.sum(window * window)


def bin_factors(kept_bins, ny):
    fine = 32
    lane = jnp.arange(2 * KY, dtype=jnp.int32)
    chunks = kept_bins.reshape(KY // BINS, 1, BINS)
    bins = jnp.concatenate([chunks, chunks], axis=1).reshape(2 * KY)
    quarter = (lane // BINS % 2) * (ny // 4)
    index = jnp.arange(fine, dtype=jnp.int32)[:, None]
    phase = jnp.stack([index * fine * bins, index * bins + quarter], 0) % ny
    angle = phase.astype(jnp.float32) * (2.0 * math.pi / ny)
    cosine, sine = jnp.cos(angle), jnp.sin(angle)
    return jnp.stack([cosine[0], sine[0], cosine[1], sine[1]], 0)


def body(pressure, centres, strides, kept_bins):
    groups = lax.axis_size("gx")
    rank = lax.axis_index("gx")
    local, nx, ny = pressure.shape
    snaps = local * groups
    half = groups // 2
    each = nx // groups
    radix = 4 if each >= 32 else 2 if each >= 16 else 1
    share = each // radix
    span = nx // radix
    signals = BANDS * OUTS

    partner = rank ^ jnp.arange(half, dtype=jnp.int32)
    times = (partner[:, None] * local + jnp.arange(local, dtype=jnp.int32)[None, :]).reshape(-1)
    factors = bin_factors(kept_bins, ny)
    bank, wsum = filter_bank(centres, strides, snaps, times)
    scale = (1.0 / (OUTS * nx * ny * wsum)).reshape(1)
    rank_word = rank.reshape(1).astype(jnp.int32)

    index = np.arange(span, dtype=np.int64)
    angle = 2.0 * np.pi * (index[:, None] * index[None, :] % span) / span
    mh, ml = split_host(np.concatenate([np.cos(angle), np.sin(-angle)], 1))
    twist = 2.0 * np.pi * (np.arange(radix)[:, None] * index[None, :]) / nx
    twist = np.broadcast_to(twist[:, :, None], (radix, span, BINS))
    twc, tws = np.cos(twist).astype(np.float32), np.sin(-twist).astype(np.float32)

    def whole(shape):
        return pl.BlockSpec(shape, lambda *_: (0,) * len(shape))

    def transform(c, factor, first, count, parts):
        sizes = [2 * share * len(part) for part in parts for _ in range(half)]
        return pl.pallas_call(
            functools.partial(transform_kernel, parts, share, groups),
            grid_spec=pltpu.PrefetchScalarGridSpec(
                num_scalar_prefetch=1,
                grid=(count,),
                in_specs=[
                    pl.BlockSpec((1, nx, ny), lambda t, _: (t + first, 0, 0)),
                    pl.BlockSpec((4, factor.shape[1], LANES), lambda t, _: (0, 0, c)),
                    whole(mh.shape),
                    whole(ml.shape),
                    whole(twc.shape),
                    whole(tws.shape),
                ],
                out_specs=[pl.BlockSpec((1, size, LANES), lambda t, _: (t, 0, 0)) for size in sizes],
                scratch_shapes=[
                    pltpu.VMEM((ny, LANES), jnp.bfloat16),
                    pltpu.VMEM((ny, LANES), jnp.bfloat16),
                    pltpu.VMEM((nx, LANES), jnp.float32),
                    pltpu.VMEM((radix, span, LANES), jnp.float32),
                ],
            ),
            out_shape=[jax.ShapeDtypeStruct((count, size, LANES), jnp.float32) for size in sizes],
            cost_estimate=pl.CostEstimate(
                flops=count * (6 * nx * ny * LANES + 12 * nx * span * LANES),
                bytes_accessed=count * nx * (ny + LANES) * 4,
                transcendentals=0,
            ),
            name="transform",
        )(rank_word, pressure, factor, mh, ml, twc, tws)

    def filtered(bank, places, pieces, side):
        total = pieces[0].shape[1] // 2
        rows = min(16, total)
        blocks = total // rows
        return pl.pallas_call(
            functools.partial(filter_kernel, places),
            grid=(blocks,),
            in_specs=[whole(bank.shape)]
            + [pl.BlockSpec((x.shape[0], rows, LANES), lambda r: (0, side * blocks + r, 0)) for x in pieces],
            out_specs=pl.BlockSpec((rows, signals, LANES), lambda r: (r, 0, 0)),
            out_shape=jax.ShapeDtypeStruct((total, signals, LANES), jnp.float32),
            scratch_shapes=[pltpu.VMEM((half * local * rows, BINS), jnp.float32)] * 2,
            cost_estimate=pl.CostEstimate(
                flops=total * 12 * signals * half * local * LANES,
                bytes_accessed=total * LANES * (half * local + signals) * 4,
                transcendentals=0,
            ),
            name="filter",
        )(bank, *pieces)

    def energy(c, parts, scale, fields, held):
        return pl.pallas_call(
            functools.partial(energy_kernel, parts, share, radix, len(held)),
            in_specs=[pl.BlockSpec(memory_space=pltpu.SMEM)]
            + [pl.BlockSpec(memory_space=pl.ANY)] * len(held)
            + [whole(x.shape) for x in fields],
            out_specs=pl.BlockSpec((BANDS, each, BINS), lambda _: (0, 0, c)),
            out_shape=jax.ShapeDtypeStruct((BANDS, each, KY), jnp.float32),
            scratch_shapes=[pltpu.VMEM((each * BANDS, BINS), jnp.float32)],
            grid=(1,),
            input_output_aliases={1: 0} if held else {},
            name="energy",
        )(scale, *held, *fields)

    def swap(value, bits):
        return lax.ppermute(value, "gx", [(i, i ^ bits) for i in range(groups)])

    def exchange(pieces):
        moved = {}
        moved.update({k: swap(pieces[k], k) for k in range(half // 2, half)})
        moved.update({k: swap(pieces[k], k) for k in range(1, half // 2)})
        return [pieces[0]] + [moved[k] for k in range(1, half)]

    last_made = [rank_word]

    def in_turn(operand):
        return lax.optimization_barrier((operand, last_made[0]))[0]

    def project(c, counts, parts):
        places, found = [], [[] for _ in parts]
        first = 0
        for count in counts:
            made = transform(c, in_turn(factors), first, count, parts)
            last_made[0] = made[0]
            places += [k * local + first for k in range(half)]
            first += count
            for q in range(len(parts)):
                found[q] += exchange(made[q * half : (q + 1) * half])
        return [(places, pieces) for pieces in found]

    def combine(group, side):
        made = filtered(in_turn(bank), *group, side)
        last_made[0] = made
        return made

    def meet(group):
        made = combine(group, 1)
        return swap(made, half)

    everything = (tuple(range(radix)),)
    (zero,) = project(0, first_counts(local), everything)
    parts = last_parts(radix)
    one = project(1, (local,), parts)
    fields = [meet(zero)]
    fields = [combine(zero, 0)] + fields
    rest, out = [], []
    for n, group in enumerate(one):
        theirs = meet(group)
        rest += [combine(group, 0), theirs]
        if n == len(one) // 2:
            out = [energy(0, everything, in_turn(scale), fields, [])]
            last_made[0] = out[0]
    return energy(1, parts, in_turn(scale), rest, out)


def first_counts(local):
    if local % 4 == 0:
        return (local // 4, local // 4, local // 2)
    return (local // 2, local // 2) if local % 2 == 0 else (local,)


def last_parts(radix):
    return {4: ((0, 1), (2,), (3,)), 2: ((0,), (1,)), 1: ((0,),)}[radix]


def solution(mesh):
    return jax.shard_map(
        body,
        mesh=mesh,
        in_specs=(P(("grp", "gx"), None, None), P(), P(), P()),
        out_specs=P("grp", "gx", None),
        check_vma=False,
    )
```

time: 406 us -> 421 us (1.037)
  waiting for transfers between devices: 179 us -> 253 us
  Pallas kernels: 153 us -> 109 us
  starting transfers between devices: 61 us -> 49.7 us
    ppermute x54 -> x46, waiting for transfers between devices: 179 us -> 253 us  [swap(): return lax.ppermute(value, 'gx', [(i, i ^ bits) for i in range(groups)])]
    pallas_call x8 -> x6, Pallas kernels: 115 us -> 78.4 us  [the longest x4 72.1 us: transform(): pl.pallas_call(functools.partial(transform_kernel, parts, share, groups),...]
    ppermute x54 -> x46, starting transfers between devices: 61 us -> 49.7 us  [swap(): return lax.ppermute(value, 'gx', [(i, i ^ bits) for i in range(groups)])]
    pallas_call x10 -> x8, Pallas kernels: 37.5 us -> 30.3 us  [filtered(): pl.pallas_call(functools.partial(filter_kernel, places), grid=(blocks,),...]
  transfers between devices with their start and end apart: 54 -> 46, of which waited for: 18 -> 28; matrix products, arithmetic and copies ran while one was open for 1% -> 1% of each run, Pallas kernels for 30% -> 19%
where the time goes in v2:
time: 421 us; the launch traced here: 420 us
  waiting for transfers between devices  253 us (60%)
  Pallas kernels  109 us (26%)
  starting transfers between devices  49.7 us (12%)
    ppermute x46, waiting for transfers between devices, swap(): return lax.ppermute(value, 'gx', [(i, i ^ bits) for i in range(groups)])  253 us
    pallas_call x4, Pallas kernels, transform(): pl.pallas_call(functools.partial(transform_kernel, parts, share, groups),...  72.1 us
    ppermute x46, starting transfers between devices, swap(): return lax.ppermute(value, 'gx', [(i, i ^ bits) for i in range(groups)])  49.7 us
    pallas_call x8, Pallas kernels, filtered(): pl.pallas_call(functools.partial(filter_kernel, places), grid=(blocks,),...  30.3 us
  transfers between devices with their start and end apart: 46, of which 28 were waited for; matrix products, arithmetic and copies ran while one was open for 1% of the time, Pallas kernels for 19%

profile of v2, /device:TPU:0, one launch (start us, length us, event | category | flops | bytes accessed | tf_op | source)
XLA Modules:
  0.0 420.1 jit_solution(3448885682910055266)
XLA Ops:
  2.1 10.8 %transform.4 = (f32[2,128,256]{2,1,0:T(8,128)}, f32[2,128,256]{2,1,0:T(8,128)}, f32[2,128,256]{2,1,0:T(8,128)}, f32[2,128,256]{2,1,0:T(8,128)}, f32[2,128,256]{2...) custom-call(s32[1]{0:T(128)} %bitcast.3.rank_ref, f32[8,1024,1024]{2,1,0:T(8,128)} %p_ref.7, ...), custom_call_target="tpu_custom_call" | custom-call | flops 4831838208 | bytes 10485760 | tf_op jit(solution)/shard_map/transform/pallas_call | solution.py:194
  13.0 10.9 %transform.5 = (f32[2,128,256]{2,1,0:T(8,128)}, f32[2,128,256]{2,1,0:T(8,128)}, f32[2,128,256]{2,1,0:T(8,128)}, f32[2,128,256]{2,1,0:T(8,128)}, f32[2,128,256]{2...) custom-call(s32[1]{0:T(128)} %bitcast.3.rank_ref, f32[8,1024,1024]{2,1,0:T(8,128)} %p_ref.7, ...), custom_call_target="tpu_custom_call" | custom-call | flops 4831838208 | bytes 10485760 | tf_op jit(solution)/shard_map/transform/pallas_call | solution.py:194
  23.9 3.1 collective-permute-start.10
  27.0 2.1 collective-permute-start.12
  30.0 17.9 %transform.6 = (f32[4,128,256]{2,1,0:T(8,128)}, f32[4,128,256]{2,1,0:T(8,128)}, f32[4,128,256]{2,1,0:T(8,128)}, f32[4,128,256]{2,1,0:T(8,128)}, f32[4,128,256]{2...) custom-call(s32[1]{0:T(128)} %bitcast.3.rank_ref, f32[8,1024,1024]{2,1,0:T(8,128)} %p_ref.7, ...), custom_call_target="tpu_custom_call" | custom-call | flops 9663676416 | bytes 20971520 | tf_op jit(solution)/shard_map/transform/pallas_call | solution.py:194
  49.6 32.4 %transform.7 = (f32[8,64,256]{2,1,0:T(8,128)}, f32[8,64,256]{2,1,0:T(8,128)}, f32[8,64,256]{2,1,0:T(8,128)}, f32[8,64,256]{2,1,0:T(8,128)}, f32[8,64,256]{2,1,0:...) custom-call(s32[1]{0:T(128)} %bitcast.3.rank_ref, ...), custom_call_target="tpu_custom_call" | custom-call | flops 19327352832 | bytes 41943040 | tf_op jit(solution)/shard_map/transform/pallas_call | solution.py:194
  86.1 4.7 %collective-permute-done.9.rest_11_ = f32[2,128,256]{2,1,0:T(8,128)S(1)} collective-permute-done((f32[2,128,256]{2,1,0:T(8,128)}, f32[2,128,256]{2,1,0:T(8,128)S(1)}, u32[]{:S(2)}, u32[]{:S(2)}) %collective-permute-start.9) | collective-permute-done | bytes 262176 | tf_op jit(solution)/shard_map/ppermute | solution.py:259
  91.9 4.9 %collective-permute-done.1.rest_2_ = f32[2,128,256]{2,1,0:T(8,128)S(1)} collective-permute-done((f32[2,128,256]{2,1,0:T(8,128)S(1)}, f32[2,128,256]{2,1,0:T(8,128)S(1)}, u32[]{:S(2)}, u32[]{:S(2)}) %collective-permute-start.1) | collective-permute-done | bytes 262176 | tf_op jit(solution)/shard_map/ppermute | solution.py:259
  97.2 4.8 %collective-permute-done.2.rest_3_ = f32[2,128,256]{2,1,0:T(8,128)S(1)} collective-permute-done((f32[2,128,256]{2,1,0:T(8,128)S(1)}, f32[2,128,256]{2,1,0:T(8,128)S(1)}, u32[]{:S(2)}, u32[]{:S(2)}) %collective-permute-start.2) | collective-permute-done | bytes 262176 | tf_op jit(solution)/shard_map/ppermute | solution.py:259
  105.8 6.6 %collective-permute-done.5.rest_6_ = f32[2,128,256]{2,1,0:T(8,128)S(1)} collective-permute-done((f32[2,128,256]{2,1,0:T(8,128)}, f32[2,128,256]{2,1,0:T(8,128)S(1)}, u32[]{:S(2)}, u32[]{:S(2)}) %collective-permute-start.5) | collective-permute-done | bytes 262176 | tf_op jit(solution)/shard_map/ppermute | solution.py:259
  113.6 3.4 collective-permute-done.6.rest_7_
  119.7 5.1 %collective-permute-done.15.rest_18_ = f32[4,128,256]{2,1,0:T(8,128)S(1)} collective-permute-done((f32[4,128,256]{2,1,0:T(8,128)}, f32[4,128,256]{2,1,0:T(8,128)S(1)}, u32[]{:S(2)}, u32[]{:S(2)}) %collective-permute-start.15) | collective-permute-done | bytes 524320 | tf_op jit(solution)/shard_map/ppermute | solution.py:259
  126.3 9.4 %collective-permute-done.16.rest_19_ = f32[4,128,256]{2,1,0:T(8,128)S(1)} collective-permute-done((f32[4,128,256]{2,1,0:T(8,128)}, f32[4,128,256]{2,1,0:T(8,128)S(1)}, u32[]{:S(2)}, u32[]{:S(2)}) %collective-permute-start.16) | collective-permute-done | bytes 524320 | tf_op jit(solution)/shard_map/ppermute | solution.py:259
  135.7 3.4 collective-permute-done.18.rest_21_
  139.1 12.5 %collective-permute-done.19.rest_22_ = f32[4,128,256]{2,1,0:T(8,128)S(1)} collective-permute-done((f32[4,128,256]{2,1,0:T(8,128)}, f32[4,128,256]{2,1,0:T(8,128)S(1)}, u32[]{:S(2)}, u32[]{:S(2)}) %collective-permute-start.19) | collective-permute-done | bytes 524320 | tf_op jit(solution)/shard_map/ppermute | solution.py:259
  151.7 10.3 %collective-permute-done.20.rest_23_ = f32[4,128,256]{2,1,0:T(8,128)} collective-permute-done((f32[4,128,256]{2,1,0:T(8,128)}, f32[4,128,256]{2,1,0:T(8,128)}, u32[]{:S(2)}, u32[]{:S(2)}) %collective-permute-start.20) | collective-permute-done | bytes 524320 | tf_op jit(solution)/shard_map/ppermute | solution.py:259
  162.0 5.9 %filter.8 = f32[64,32,256]{2,1,0:T(8,128)} custom-call(bf16[64,128]{1,0:T(8,128)(2,1)} %pad_maximum_fusion.2.bank_ref, f32[2,128,256]{2,1,0:T(8,128)} %get-tuple-element.68.rest_0_, f32[2,128,256]{2,1,0:T(8,128)} %copy-done.19, f32[2,128,256]{2,1,0:T(8,128)} %copy-done.20, f32[2,128,256]{2,1,0:T(8,128)} %copy-done.21, f32[2,128,256]{2,1,0:T(8,128)} %copy-done.22, ...), custom_call_target="tpu_custom_call" | custom-call | flops 402653184 | bytes 6291456 | tf_op jit(solution)/shard_map/filter/pallas_call | solution.py:228
  168.0 2.7 collective-permute-start.35
  172.5 2.0 collective-permute-start.31
  174.5 5.6 %collective-permute-done.29.rest_2_ = f32[8,32,256]{2,1,0:T(8,128)S(1)} collective-permute-done((f32[8,32,256]{2,1,0:T(8,128)}, f32[8,32,256]{2,1,0:T(8,128)S(1)}, u32[]{:S(2)}, u32[]{:S(2)}) %collective-permute-start.29) | collective-permute-done | bytes 262176 | tf_op jit(solution)/shard_map/ppermute | solution.py:259
  180.1 4.6 %collective-permute-done.30.rest_3_ = f32[8,32,256]{2,1,0:T(8,128)S(1)} collective-permute-done((f32[8,32,256]{2,1,0:T(8,128)}, f32[8,32,256]{2,1,0:T(8,128)S(1)}, u32[]{:S(2)}, u32[]{:S(2)}) %collective-permute-start.30) | collective-permute-done | bytes 262176 | tf_op jit(solution)/shard_map/ppermute | solution.py:259
  186.6 36.0 %collective-permute-done.31.rest_4_ = f32[8,32,256]{2,1,0:T(8,128)S(1)} collective-permute-done((f32[8,32,256]{2,1,0:T(8,128)}, f32[8,32,256]{2,1,0:T(8,128)S(1)}, u32[]{:S(2)}, u32[]{:S(2)}) %collective-permute-start.31) | collective-permute-done | bytes 262176 | tf_op jit(solution)/shard_map/ppermute | solution.py:259
  223.3 4.3 %collective-permute-done.32.rest_5_ = f32[8,32,256]{2,1,0:T(8,128)S(1)} collective-permute-done((f32[8,32,256]{2,1,0:T(8,128)}, f32[8,32,256]{2,1,0:T(8,128)S(1)}, u32[]{:S(2)}, u32[]{:S(2)}) %collective-permute-start.32) | collective-permute-done | bytes 262176 | tf_op jit(solution)/shard_map/ppermute | solution.py:259
  227.6 1.9 collective-permute-start.33
  229.5 38.4 %collective-permute-done.33.rest_6_ = f32[8,32,256]{2,1,0:T(8,128)S(1)} collective-permute-done((f32[8,32,256]{2,1,0:T(8,128)}, f32[8,32,256]{2,1,0:T(8,128)S(1)}, u32[]{:S(2)}, u32[]{:S(2)}) %collective-permute-start.33) | collective-permute-done | bytes 262176 | tf_op jit(solution)/shard_map/ppermute | solution.py:259
  273.1 10.6 %collective-permute-done.24.rest_4_ = f32[8,64,256]{2,1,0:T(8,128)S(1)} collective-permute-done((f32[8,64,256]{2,1,0:T(8,128)}, f32[8,64,256]{2,1,0:T(8,128)S(1)}, u32[]{:S(2)}, u32[]{:S(2)}) %collective-permute-start.24) | collective-permute-done | bytes 524320 | tf_op jit(solution)/shard_map/ppermute | solution.py:259
  283.7 6.1 %filter.9.rest_0_ = f32[64,32,256]{2,1,0:T(8,128)} custom-call(bf16[64,128]{1,0:T(8,128)(2,1)} %pad_maximum_fusion.2.bank_ref, f32[2,128,256]{2,1,0:T(8,128)} %get-tuple-element.68.rest_0_, f32[2,128,256]{2,1,0:T(8,128)} %copy-done.19, f32[2,128,256]{2,1,0:T(8,128)} %copy-done.20, f32[2,128,256]{2,1,0:T(8,128)} %copy-done.21, f32[2,128,256]{2,1,0:T(8,128)} %copy-done.22, ...), custom_call_target="tpu_custom_call" | custom-call | flops 402653184 | bytes 6291456 | tf_op jit(solution)/shard_map/filter/pallas_call | solution.py:228
  289.8 3.3 collective-permute-done.25.rest_5_
  294.7 11.9 %collective-permute-done.26.rest_6_ = f32[8,64,256]{2,1,0:T(8,128)S(1)} collective-permute-done((f32[8,64,256]{2,1,0:T(8,128)}, f32[8,64,256]{2,1,0:T(8,128)S(1)}, u32[]{:S(2)}, u32[]{:S(2)}) %collective-permute-start.26) | collective-permute-done | bytes 524320 | tf_op jit(solution)/shard_map/ppermute | solution.py:259
  307.6 8.7 %collective-permute-done.27.rest_7_ = f32[8,64,256]{2,1,0:T(8,128)} collective-permute-done((f32[8,64,256]{2,1,0:T(8,128)}, f32[8,64,256]{2,1,0:T(8,128)}, u32[]{:S(2)}, u32[]{:S(2)}) %collective-permute-start.27) | collective-permute-done | bytes 524320 | tf_op jit(solution)/shard_map/ppermute | solution.py:259
  316.3 2.4 collective-permute-start.38
  318.7 3.6 filter.10
  322.3 2.3 collective-permute-start.43
  328.3 5.4 %collective-permute-done.38.rest_3_ = f32[8,32,256]{2,1,0:T(8,128)S(1)} collective-permute-done((f32[8,32,256]{2,1,0:T(8,128)}, f32[8,32,256]{2,1,0:T(8,128)S(1)}, u32[]{:S(2)}, u32[]{:S(2)}) %collective-permute-start.38) | collective-permute-done | bytes 262176 | tf_op jit(solution)/shard_map/ppermute | solution.py:259
  337.6 3.5 filter.11.rest_1_
  341.1 2.8 filter.12
  343.9 2.8 filter.13.rest_3_
  346.8 3.2 energy.2.rest_0_
  350.0 4.0 collective-permute-done.39.rest_4_
  354.0 2.2 collective-permute-start.44
  356.2 3.5 collective-permute-done.40.rest_5_
  359.7 5.6 %collective-permute-done.41.rest_6_ = f32[8,32,256]{2,1,0:T(8,128)S(1)} collective-permute-done((f32[8,32,256]{2,1,0:T(8,128)}, f32[8,32,256]{2,1,0:T(8,128)S(1)}, u32[]{:S(2)}, u32[]{:S(2)}) %collective-permute-start.41) | collective-permute-done | bytes 262176 | tf_op jit(solution)/shard_map/ppermute | solution.py:259
  365.3 5.6 %collective-permute-done.42.rest_7_ = f32[8,32,256]{2,1,0:T(8,128)S(1)} collective-permute-done((f32[8,32,256]{2,1,0:T(8,128)}, f32[8,32,256]{2,1,0:T(8,128)S(1)}, u32[]{:S(2)}, u32[]{:S(2)}) %collective-permute-start.42) | collective-permute-done | bytes 262176 | tf_op jit(solution)/shard_map/ppermute | solution.py:259
  371.7 2.8 filter.14
  375.8 2.8 filter.15.rest_5_
  378.6 27.1 %collective-permute-done.44.rest_4_ = f32[16,32,256]{2,1,0:T(8,128)S(1)} collective-permute-done((f32[16,32,256]{2,1,0:T(8,128)S(1)}, f32[16,32,256]{2,1,0:T(8,128)S(1)}, u32[]{:S(2)}, u32[]{:S(2)}) %collective-permute-start.44) | collective-permute-done | bytes 524320 | tf_op jit(solution)/shard_map/ppermute | solution.py:259
  405.7 10.5 %collective-permute-done.45.rest_6_ = f32[16,32,256]{2,1,0:T(8,128)S(1)} collective-permute-done((f32[16,32,256]{2,1,0:T(8,128)}, f32[16,32,256]{2,1,0:T(8,128)S(1)}, u32[]{:S(2)}, u32[]{:S(2)}) %collective-permute-start.45) | collective-permute-done | bytes 524320 | tf_op jit(solution)/shard_map/ppermute | solution.py:259
  417.0 3.1 energy.3
  (178 shorter events, 41.3 us)
Async XLA Ops:
  23.9 24.1 %collective-permute-start.10 = (f32[2,128,256]{2,1,0:T(8,128)}, f32[2,128,256]{2,1,0:T(8,128)S(1)}, u32[]{:S(2)}, u32[]{:S(2)}) collective-permute-start(f32[2,128,256]{2,1,0:T(8,128)} %get-tuple-element.86), channel_id=1, source_target_pairs={{0,4},{1,5},{2,6},{3,7},{4,0},{5,1},{6,2},{7,3},{8,12},{9,13},{10,... | collective-permute-start | bytes 786440 | tf_op jit(solution)/shard_map/ppermute | solution.py:259
  27.0 55.1 %collective-permute-start.11 = (f32[2,128,256]{2,1,0:T(8,128)}, f32[2,128,256]{2,1,0:T(8,128)S(1)}, u32[]{:S(2)}, u32[]{:S(2)}) collective-permute-start(f32[2,128,256]{2,1,0:T(8,128)} %get-tuple-element.87), channel_id=1, source_target_pairs={{0,5},{1,4},{2,7},{3,6},{4,1},{5,0},{6,3},{7,2},{8,13},{9,12},{10,... | collective-permute-start | bytes 786440 | tf_op jit(solution)/shard_map/ppermute | solution.py:259
  27.0 55.3 %collective-permute-start.12 = (f32[2,128,256]{2,1,0:T(8,128)}, f32[2,128,256]{2,1,0:T(8,128)S(1)}, u32[]{:S(2)}, u32[]{:S(2)}) collective-permute-start(f32[2,128,256]{2,1,0:T(8,128)} %get-tuple-element.88), channel_id=1, source_target_pairs={{0,6},{1,7},{2,4},{3,5},{4,2},{5,3},{6,0},{7,1},{8,14},{9,15},{10,... | collective-permute-start | bytes 786440 | tf_op jit(solution)/shard_map/ppermute | solution.py:259
  29.1 53.7 %collective-permute-start.13 = (f32[2,128,256]{2,1,0:T(8,128)}, f32[2,128,256]{2,1,0:T(8,128)S(1)}, u32[]{:S(2)}, u32[]{:S(2)}) collective-permute-start(f32[2,128,256]{2,1,0:T(8,128)} %get-tuple-element.89), channel_id=1, source_target_pairs={{0,7},{1,6},{2,5},{3,4},{4,3},{5,2},{6,1},{7,0},{8,15},{9,14},{10,... | collective-permute-start | bytes 786440 | tf_op jit(solution)/shard_map/ppermute | solution.py:259
  29.7 54.7 %collective-permute-start.7 = (f32[2,128,256]{2,1,0:T(8,128)}, f32[2,128,256]{2,1,0:T(8,128)S(1)}, u32[]{:S(2)}, u32[]{:S(2)}) collective-permute-start(f32[2,128,256]{2,1,0:T(8,128)} %get-tuple-element.83), channel_id=1, source_target_pairs={{0,1},{1,0},{2,3},{3,2},{4,5},{5,4},{6,7},{7,6},{8,9},{9,8},{10,11... | collective-permute-start | bytes 786440 | tf_op jit(solution)/shard_map/ppermute | solution.py:259
  48.0 36.5 %collective-permute-start.8 = (f32[2,128,256]{2,1,0:T(8,128)S(1)}, f32[2,128,256]{2,1,0:T(8,128)S(1)}, u32[]{:S(2)}, u32[]{:S(2)}) collective-permute-start(f32[2,128,256]{2,1,0:T(8,128)S(1)} %copy-done.49), channel_id=1, source_target_pairs={{0,2},{1,3},{2,0},{3,1},{4,6},{5,7},{6,4},{7,5},{8,10},{9,11},{10,... | collective-permute-start | bytes 786440 | tf_op jit(solution)/shard_map/ppermute | solution.py:259
  82.1 8.7 %collective-permute-start.9 = (f32[2,128,256]{2,1,0:T(8,128)}, f32[2,128,256]{2,1,0:T(8,128)S(1)}, u32[]{:S(2)}, u32[]{:S(2)}) collective-permute-start(f32[2,128,256]{2,1,0:T(8,128)} %get-tuple-element.85), channel_id=1, source_target_pairs={{0,3},{1,2},{2,1},{3,0},{4,7},{5,6},{6,5},{7,4},{8,11},{9,10},{10,... | collective-permute-start | bytes 786440 | tf_op jit(solution)/shard_map/ppermute | solution.py:259
  82.2 9.1 %collective-permute-start = (f32[2,128,256]{2,1,0:T(8,128)}, f32[2,128,256]{2,1,0:T(8,128)S(1)}, u32[]{:S(2)}, u32[]{:S(2)}) collective-permute-start(f32[2,128,256]{2,1,0:T(8,128)} %get-tuple-element.76), channel_id=1, source_target_pairs={{0,1},{1,0},{2,3},{3,2},{4,5},{5,4},{6,7},{7,6},{8,9},{9,8},{10,11... | collective-permute-start | bytes 786440 | tf_op jit(solution)/shard_map/ppermute | solution.py:259
  82.8 13.9 %collective-permute-start.1 = (f32[2,128,256]{2,1,0:T(8,128)S(1)}, f32[2,128,256]{2,1,0:T(8,128)S(1)}, u32[]{:S(2)}, u32[]{:S(2)}) collective-permute-start(f32[2,128,256]{2,1,0:T(8,128)S(1)} %copy-done.48), channel_id=1, source_target_pairs={{0,2},{1,3},{2,0},{3,1},{4,6},{5,7},{6,4},{7,5},{8,10},{9,11},{10,... | collective-permute-start | bytes 786440 | tf_op jit(solution)/shard_map/ppermute | solution.py:259
  84.4 17.6 %collective-permute-start.2 = (f32[2,128,256]{2,1,0:T(8,128)S(1)}, f32[2,128,256]{2,1,0:T(8,128)S(1)}, u32[]{:S(2)}, u32[]{:S(2)}) collective-permute-start(f32[2,128,256]{2,1,0:T(8,128)S(1)} %copy-done.47), channel_id=1, source_target_pairs={{0,3},{1,2},{2,1},{3,0},{4,7},{5,6},{6,5},{7,4},{8,11},{9,10},{10,... | collective-permute-start | bytes 786440 | tf_op jit(solution)/shard_map/ppermute | solution.py:259
  84.5 18.5 %collective-permute-start.3 = (f32[2,128,256]{2,1,0:T(8,128)S(1)}, f32[2,128,256]{2,1,0:T(8,128)S(1)}, u32[]{:S(2)}, u32[]{:S(2)}) collective-permute-start(f32[2,128,256]{2,1,0:T(8,128)S(1)} %copy-done.46), channel_id=1, source_target_pairs={{0,4},{1,5},{2,6},{3,7},{4,0},{5,1},{6,2},{7,3},{8,12},{9,13},{10,... | collective-permute-start | bytes 786440 | tf_op jit(solution)/shard_map/ppermute | solution.py:259
  90.8 28.0 %collective-permute-start.14 = (f32[4,128,256]{2,1,0:T(8,128)}, f32[4,128,256]{2,1,0:T(8,128)S(1)}, u32[]{:S(2)}, u32[]{:S(2)}) collective-permute-start(f32[4,128,256]{2,1,0:T(8,128)} %get-tuple-element.90), channel_id=1, source_target_pairs={{0,1},{1,0},{2,3},{3,2},{4,5},{5,4},{6,7},{7,6},{8,9},{9,8},{10,11... | collective-permute-start | bytes 1572872 | tf_op jit(solution)/shard_map/ppermute | solution.py:259
  91.3 33.5 %collective-permute-start.15 = (f32[4,128,256]{2,1,0:T(8,128)}, f32[4,128,256]{2,1,0:T(8,128)S(1)}, u32[]{:S(2)}, u32[]{:S(2)}) collective-permute-start(f32[4,128,256]{2,1,0:T(8,128)} %get-tuple-element.91), channel_id=1, source_target_pairs={{0,2},{1,3},{2,0},{3,1},{4,6},{5,7},{6,4},{7,5},{8,10},{9,11},{10,... | collective-permute-start | bytes 1572872 | tf_op jit(solution)/shard_map/ppermute | solution.py:259
  96.7 8.7 %collective-permute-start.4 = (f32[2,128,256]{2,1,0:T(8,128)}, f32[2,128,256]{2,1,0:T(8,128)S(1)}, u32[]{:S(2)}, u32[]{:S(2)}) collective-permute-start(f32[2,128,256]{2,1,0:T(8,128)} %get-tuple-element.80), channel_id=1, source_target_pairs={{0,5},{1,4},{2,7},{3,6},{4,1},{5,0},{6,3},{7,2},{8,13},{9,12},{10,... | collective-permute-start | bytes 786440 | tf_op jit(solution)/shard_map/ppermute | solution.py:259
  102.0 10.4 %collective-permute-start.5 = (f32[2,128,256]{2,1,0:T(8,128)}, f32[2,128,256]{2,1,0:T(8,128)S(1)}, u32[]{:S(2)}, u32[]{:S(2)}) collective-permute-start(f32[2,128,256]{2,1,0:T(8,128)} %get-tuple-element.81), channel_id=1, source_target_pairs={{0,6},{1,7},{2,4},{3,5},{4,2},{5,3},{6,0},{7,1},{8,14},{9,15},{10,... | collective-permute-start | bytes 786440 | tf_op jit(solution)/shard_map/ppermute | solution.py:259
  103.1 13.9 %collective-permute-start.6 = (f32[2,128,256]{2,1,0:T(8,128)}, f32[2,128,256]{2,1,0:T(8,128)S(1)}, u32[]{:S(2)}, u32[]{:S(2)}) collective-permute-start(f32[2,128,256]{2,1,0:T(8,128)} %get-tuple-element.82), channel_id=1, source_target_pairs={{0,7},{1,6},{2,5},{3,4},{4,3},{5,2},{6,1},{7,0},{8,15},{9,14},{10,... | collective-permute-start | bytes 786440 | tf_op jit(solution)/shard_map/ppermute | solution.py:259
  105.4 30.3 %collective-permute-start.16 = (f32[4,128,256]{2,1,0:T(8,128)}, f32[4,128,256]{2,1,0:T(8,128)S(1)}, u32[]{:S(2)}, u32[]{:S(2)}) collective-permute-start(f32[4,128,256]{2,1,0:T(8,128)} %get-tuple-element.92), channel_id=1, source_target_pairs={{0,3},{1,2},{2,1},{3,0},{4,7},{5,6},{6,5},{7,4},{8,11},{9,10},{10,... | collective-permute-start | bytes 1572872 | tf_op jit(solution)/shard_map/ppermute | solution.py:259
  112.4 23.3 %collective-permute-start.17 = (f32[4,128,256]{2,1,0:T(8,128)}, f32[4,128,256]{2,1,0:T(8,128)S(1)}, u32[]{:S(2)}, u32[]{:S(2)}) collective-permute-start(f32[4,128,256]{2,1,0:T(8,128)} %get-tuple-element.93), channel_id=1, source_target_pairs={{0,4},{1,5},{2,6},{3,7},{4,0},{5,1},{6,2},{7,3},{8,12},{9,13},{10,... | collective-permute-start | bytes 1572872 | tf_op jit(solution)/shard_map/ppermute | solution.py:259
  117.0 22.1 %collective-permute-start.18 = (f32[4,128,256]{2,1,0:T(8,128)}, f32[4,128,256]{2,1,0:T(8,128)S(1)}, u32[]{:S(2)}, u32[]{:S(2)}) collective-permute-start(f32[4,128,256]{2,1,0:T(8,128)} %get-tuple-element.94), channel_id=1, source_target_pairs={{0,5},{1,4},{2,7},{3,6},{4,1},{5,0},{6,3},{7,2},{8,13},{9,12},{10,... | collective-permute-start | bytes 1572872 | tf_op jit(solution)/shard_map/ppermute | solution.py:259
  118.8 32.9 %collective-permute-start.19 = (f32[4,128,256]{2,1,0:T(8,128)}, f32[4,128,256]{2,1,0:T(8,128)S(1)}, u32[]{:S(2)}, u32[]{:S(2)}) collective-permute-start(f32[4,128,256]{2,1,0:T(8,128)} %get-tuple-element.95), channel_id=1, source_target_pairs={{0,6},{1,7},{2,4},{3,5},{4,2},{5,3},{6,0},{7,1},{8,14},{9,15},{10,... | collective-permute-start | bytes 1572872 | tf_op jit(solution)/shard_map/ppermute | solution.py:259
  124.8 37.2 %collective-permute-start.20 = (f32[4,128,256]{2,1,0:T(8,128)}, f32[4,128,256]{2,1,0:T(8,128)}, u32[]{:S(2)}, u32[]{:S(2)}) collective-permute-start(f32[4,128,256]{2,1,0:T(8,128)} %get-tuple-element.96), channel_id=1, source_target_pairs={{0,7},{1,6},{2,5},{3,4},{4,3},{5,2},{6,1},{7,0},{8,15},{9,14},{10,... | collective-permute-start | bytes 1572872 | tf_op jit(solution)/shard_map/ppermute | solution.py:259
  168.0 166.4 %collective-permute-start.35 = (f32[64,32,256]{2,1,0:T(8,128)}, f32[64,32,256]{2,1,0:T(8,128)}, u32[]{:S(2)}, u32[]{:S(2)}) collective-permute-start(f32[64,32,256]{2,1,0:T(8,128)} %filter.8), channel_id=1, source_target_pairs={{0,8},{1,9},{2,10},{3,11},{4,12},{5,13},{6,14},{7,15},{8,0},{9,1},... | collective-permute-start | bytes 6291464 | tf_op jit(solution)/shard_map/ppermute | solution.py:259
  170.6 3.9 collective-permute-start.28
  170.7 9.4 %collective-permute-start.29 = (f32[8,32,256]{2,1,0:T(8,128)}, f32[8,32,256]{2,1,0:T(8,128)S(1)}, u32[]{:S(2)}, u32[]{:S(2)}) collective-permute-start(f32[8,32,256]{2,1,0:T(8,128)} %get-tuple-element.110), channel_id=1, source_target_pairs={{0,2},{1,3},{2,0},{3,1},{4,6},{5,7},{6,4},{7,5},{8,10},{9,11},{10,... | collective-permute-start | bytes 786440 | tf_op jit(solution)/shard_map/ppermute | solution.py:259
  171.8 12.9 %collective-permute-start.30 = (f32[8,32,256]{2,1,0:T(8,128)}, f32[8,32,256]{2,1,0:T(8,128)S(1)}, u32[]{:S(2)}, u32[]{:S(2)}) collective-permute-start(f32[8,32,256]{2,1,0:T(8,128)} %get-tuple-element.111), channel_id=1, source_target_pairs={{0,3},{1,2},{2,1},{3,0},{4,7},{5,6},{6,5},{7,4},{8,11},{9,10},{10,... | collective-permute-start | bytes 786440 | tf_op jit(solution)/shard_map/ppermute | solution.py:259
  172.5 50.1 %collective-permute-start.31 = (f32[8,32,256]{2,1,0:T(8,128)}, f32[8,32,256]{2,1,0:T(8,128)S(1)}, u32[]{:S(2)}, u32[]{:S(2)}) collective-permute-start(f32[8,32,256]{2,1,0:T(8,128)} %get-tuple-element.112), channel_id=1, source_target_pairs={{0,4},{1,5},{2,6},{3,7},{4,0},{5,1},{6,2},{7,3},{8,12},{9,13},{10,... | collective-permute-start | bytes 786440 | tf_op jit(solution)/shard_map/ppermute | solution.py:259
  174.5 115.2 %copy-start.26 = (f32[8,32,256]{2,1,0:T(8,128)}, f32[8,32,256]{2,1,0:T(8,128)S(1)}, u32[]{:S(2)}) copy-start(f32[8,32,256]{2,1,0:T(8,128)S(1)} %collective-permute-done.28.rest_1_) | copy-start | bytes 786436
  174.5 53.1 %collective-permute-start.32 = (f32[8,32,256]{2,1,0:T(8,128)}, f32[8,32,256]{2,1,0:T(8,128)S(1)}, u32[]{:S(2)}, u32[]{:S(2)}) collective-permute-start(f32[8,32,256]{2,1,0:T(8,128)} %get-tuple-element.113), channel_id=1, source_target_pairs={{0,5},{1,4},{2,7},{3,6},{4,1},{5,0},{6,3},{7,2},{8,13},{9,12},{10,... | collective-permute-start | bytes 786440 | tf_op jit(solution)/shard_map/ppermute | solution.py:259
  180.1 103.6 %copy-start.27 = (f32[8,32,256]{2,1,0:T(8,128)}, f32[8,32,256]{2,1,0:T(8,128)S(1)}, u32[]{:S(2)}) copy-start(f32[8,32,256]{2,1,0:T(8,128)S(1)} %collective-permute-done.29.rest_2_) | copy-start | bytes 786436
  180.1 88.6 %collective-permute-start.21 = (f32[8,64,256]{2,1,0:T(8,128)}, f32[8,64,256]{2,1,0:T(8,128)S(1)}, u32[]{:S(2)}, u32[]{:S(2)}) collective-permute-start(f32[8,64,256]{2,1,0:T(8,128)} %get-tuple-element.99), channel_id=1, source_target_pairs={{0,1},{1,0},{2,3},{3,2},{4,5},{5,4},{6,7},{7,6},{8,9},{9,8},{10,11... | collective-permute-start | bytes 1572872 | tf_op jit(solution)/shard_map/ppermute | solution.py:259
  185.4 84.7 %collective-permute-start.22 = (f32[8,64,256]{2,1,0:T(8,128)}, f32[8,64,256]{2,1,0:T(8,128)S(1)}, u32[]{:S(2)}, u32[]{:S(2)}) collective-permute-start(f32[8,64,256]{2,1,0:T(8,128)} %get-tuple-element.100), channel_id=1, source_target_pairs={{0,2},{1,3},{2,0},{3,1},{4,6},{5,7},{6,4},{7,5},{8,10},{9,11},{10,... | collective-permute-start | bytes 1572872 | tf_op jit(solution)/shard_map/ppermute | solution.py:259
  223.3 48.0 %collective-permute-start.23 = (f32[8,64,256]{2,1,0:T(8,128)}, f32[8,64,256]{2,1,0:T(8,128)S(1)}, u32[]{:S(2)}, u32[]{:S(2)}) collective-permute-start(f32[8,64,256]{2,1,0:T(8,128)} %get-tuple-element.101), channel_id=1, source_target_pairs={{0,3},{1,2},{2,1},{3,0},{4,7},{5,6},{6,5},{7,4},{8,11},{9,10},{10,... | collective-permute-start | bytes 1572872 | tf_op jit(solution)/shard_map/ppermute | solution.py:259
  227.6 40.4 %collective-permute-start.33 = (f32[8,32,256]{2,1,0:T(8,128)}, f32[8,32,256]{2,1,0:T(8,128)S(1)}, u32[]{:S(2)}, u32[]{:S(2)}) collective-permute-start(f32[8,32,256]{2,1,0:T(8,128)} %get-tuple-element.114), channel_id=1, source_target_pairs={{0,6},{1,7},{2,4},{3,5},{4,2},{5,3},{6,0},{7,1},{8,14},{9,15},{10,... | collective-permute-start | bytes 786440 | tf_op jit(solution)/shard_map/ppermute | solution.py:259
  268.7 15.0 %collective-permute-start.24 = (f32[8,64,256]{2,1,0:T(8,128)}, f32[8,64,256]{2,1,0:T(8,128)S(1)}, u32[]{:S(2)}, u32[]{:S(2)}) collective-permute-start(f32[8,64,256]{2,1,0:T(8,128)} %get-tuple-element.102), channel_id=1, source_target_pairs={{0,4},{1,5},{2,6},{3,7},{4,0},{5,1},{6,2},{7,3},{8,12},{9,13},{10,... | collective-permute-start | bytes 1572872 | tf_op jit(solution)/shard_map/ppermute | solution.py:259
  268.7 24.4 %collective-permute-start.25 = (f32[8,64,256]{2,1,0:T(8,128)}, f32[8,64,256]{2,1,0:T(8,128)S(1)}, u32[]{:S(2)}, u32[]{:S(2)}) collective-permute-start(f32[8,64,256]{2,1,0:T(8,128)} %get-tuple-element.103), channel_id=1, source_target_pairs={{0,5},{1,4},{2,7},{3,6},{4,1},{5,0},{6,3},{7,2},{8,13},{9,12},{10,... | collective-permute-start | bytes 1572872 | tf_op jit(solution)/shard_map/ppermute | solution.py:259
  270.1 36.6 %collective-permute-start.26 = (f32[8,64,256]{2,1,0:T(8,128)}, f32[8,64,256]{2,1,0:T(8,128)S(1)}, u32[]{:S(2)}, u32[]{:S(2)}) collective-permute-start(f32[8,64,256]{2,1,0:T(8,128)} %get-tuple-element.104), channel_id=1, source_target_pairs={{0,6},{1,7},{2,4},{3,5},{4,2},{5,3},{6,0},{7,1},{8,14},{9,15},{10,... | collective-permute-start | bytes 1572872 | tf_op jit(solution)/shard_map/ppermute | solution.py:259
  271.3 45.0 %collective-permute-start.27 = (f32[8,64,256]{2,1,0:T(8,128)}, f32[8,64,256]{2,1,0:T(8,128)}, u32[]{:S(2)}, u32[]{:S(2)}) collective-permute-start(f32[8,64,256]{2,1,0:T(8,128)} %get-tuple-element.105), channel_id=1, source_target_pairs={{0,7},{1,6},{2,5},{3,4},{4,3},{5,2},{6,1},{7,0},{8,15},{9,14},{10,... | collective-permute-start | bytes 1572872 | tf_op jit(solution)/shard_map/ppermute | solution.py:259
  283.7 38.6 %collective-permute-start.34 = (f32[8,32,256]{2,1,0:T(8,128)}, f32[8,32,256]{2,1,0:T(8,128)}, u32[]{:S(2)}, u32[]{:S(2)}) collective-permute-start(f32[8,32,256]{2,1,0:T(8,128)} %get-tuple-element.115), channel_id=1, source_target_pairs={{0,7},{1,6},{2,5},{3,4},{4,3},{5,2},{6,1},{7,0},{8,15},{9,14},{10,... | collective-permute-start | bytes 786440 | tf_op jit(solution)/shard_map/ppermute | solution.py:259
  293.1 31.5 %collective-permute-start.36 = (f32[8,32,256]{2,1,0:T(8,128)}, f32[8,32,256]{2,1,0:T(8,128)S(1)}, u32[]{:S(2)}, u32[]{:S(2)}) collective-permute-start(f32[8,32,256]{2,1,0:T(8,128)} %get-tuple-element.120), channel_id=1, source_target_pairs={{0,1},{1,0},{2,3},{3,2},{4,5},{5,4},{6,7},{7,6},{8,9},{9,8},{10,11... | collective-permute-start | bytes 786440 | tf_op jit(solution)/shard_map/ppermute | solution.py:259
  306.6 21.7 %collective-permute-start.37 = (f32[8,32,256]{2,1,0:T(8,128)}, f32[8,32,256]{2,1,0:T(8,128)S(1)}, u32[]{:S(2)}, u32[]{:S(2)}) collective-permute-start(f32[8,32,256]{2,1,0:T(8,128)} %get-tuple-element.121), channel_id=1, source_target_pairs={{0,2},{1,3},{2,0},{3,1},{4,6},{5,7},{6,4},{7,5},{8,10},{9,11},{10,... | collective-permute-start | bytes 786440 | tf_op jit(solution)/shard_map/ppermute | solution.py:259
  316.3 17.5 %collective-permute-start.38 = (f32[8,32,256]{2,1,0:T(8,128)}, f32[8,32,256]{2,1,0:T(8,128)S(1)}, u32[]{:S(2)}, u32[]{:S(2)}) collective-permute-start(f32[8,32,256]{2,1,0:T(8,128)} %get-tuple-element.122), channel_id=1, source_target_pairs={{0,3},{1,2},{2,1},{3,0},{4,7},{5,6},{6,5},{7,4},{8,11},{9,10},{10,... | collective-permute-start | bytes 786440 | tf_op jit(solution)/shard_map/ppermute | solution.py:259
  322.3 83.4 %collective-permute-start.43 = (f32[32,32,256]{2,1,0:T(8,128)}, f32[32,32,256]{2,1,0:T(8,128)S(1)}, u32[]{:S(2)}, u32[]{:S(2)}) collective-permute-start(f32[32,32,256]{2,1,0:T(8,128)} %filter.10), channel_id=1, source_target_pairs={{0,8},{1,9},{2,10},{3,11},{4,12},{5,13},{6,14},{7,15},{8,0},{9,1},... | collective-permute-start | bytes 3145736 | tf_op jit(solution)/shard_map/ppermute | solution.py:259
  324.6 29.4 %collective-permute-start.39 = (f32[8,32,256]{2,1,0:T(8,128)S(1)}, f32[8,32,256]{2,1,0:T(8,128)S(1)}, u32[]{:S(2)}, u32[]{:S(2)}) collective-permute-start(f32[8,32,256]{2,1,0:T(8,128)S(1)} %copy-done.45), channel_id=1, source_target_pairs={{0,4},{1,5},{2,6},{3,7},{4,0},{5,1},{6,2},{7,3},{8,12},{9,13},{10,... | collective-permute-start | bytes 786440 | tf_op jit(solution)/shard_map/ppermute | solution.py:259
  328.3 31.4 %collective-permute-start.40 = (f32[8,32,256]{2,1,0:T(8,128)}, f32[8,32,256]{2,1,0:T(8,128)S(1)}, u32[]{:S(2)}, u32[]{:S(2)}) collective-permute-start(f32[8,32,256]{2,1,0:T(8,128)} %get-tuple-element.124), channel_id=1, source_target_pairs={{0,5},{1,4},{2,7},{3,6},{4,1},{5,0},{6,3},{7,2},{8,13},{9,12},{10,... | collective-permute-start | bytes 786440 | tf_op jit(solution)/shard_map/ppermute | solution.py:259
  333.7 31.6 %collective-permute-start.41 = (f32[8,32,256]{2,1,0:T(8,128)}, f32[8,32,256]{2,1,0:T(8,128)S(1)}, u32[]{:S(2)}, u32[]{:S(2)}) collective-permute-start(f32[8,32,256]{2,1,0:T(8,128)} %get-tuple-element.125), channel_id=1, source_target_pairs={{0,6},{1,7},{2,4},{3,5},{4,2},{5,3},{6,0},{7,1},{8,14},{9,15},{10,... | collective-permute-start | bytes 786440 | tf_op jit(solution)/shard_map/ppermute | solution.py:259
  334.4 36.5 %collective-permute-start.42 = (f32[8,32,256]{2,1,0:T(8,128)}, f32[8,32,256]{2,1,0:T(8,128)S(1)}, u32[]{:S(2)}, u32[]{:S(2)}) collective-permute-start(f32[8,32,256]{2,1,0:T(8,128)} %get-tuple-element.126), channel_id=1, source_target_pairs={{0,7},{1,6},{2,5},{3,4},{4,3},{5,2},{6,1},{7,0},{8,15},{9,14},{10,... | collective-permute-start | bytes 786440 | tf_op jit(solution)/shard_map/ppermute | solution.py:259
  354.0 51.7 %collective-permute-start.44 = (f32[16,32,256]{2,1,0:T(8,128)S(1)}, f32[16,32,256]{2,1,0:T(8,128)S(1)}, u32[]{:S(2)}, u32[]{:S(2)}) collective-permute-start(f32[16,32,256]{2,1,0:T(8,128)S(1)} %copy-done.40), channel_id=1, source_target_pairs={{0,8},{1,9},{2,10},{3,11},{4,12},{5,13},{6,14},{7,15},{8,0},{9,1},... | collective-permute-start | bytes 1572872 | tf_op jit(solution)/shard_map/ppermute | solution.py:259
  374.4 41.7 %collective-permute-start.45 = (f32[16,32,256]{2,1,0:T(8,128)}, f32[16,32,256]{2,1,0:T(8,128)S(1)}, u32[]{:S(2)}, u32[]{:S(2)}) collective-permute-start(f32[16,32,256]{2,1,0:T(8,128)} %filter.14), channel_id=1, source_target_pairs={{0,8},{1,9},{2,10},{3,11},{4,12},{5,13},{6,14},{7,15},{8,0},{9,1},... | collective-permute-start | bytes 1572872 | tf_op jit(solution)/shard_map/ppermute | solution.py:259
  (48 other events, 874.0 us)
